TPU v7x, 32 devices: a whole 2x2x4 slice. The times are simulated.
32 devices in a mesh: rep: 2 (over core), row: 4 (over z), tp: 4 (over y, x).
Axes of the slice: x: 2, y: 2, z: 4, core: 2. Of those that a mesh axis runs over, the one named last changes fastest.
Arguments:
- entry_gradient: bfloat16 [2, 8, 640, 5632], P('rep', None, 'row', 'tp'), may hold values from -900 to 900
- exit_gradient: bfloat16 [2, 8, 3072, 640], P('rep', None, 'row', 'tp'), may hold values from -900 to 900
- embed_gradient: bfloat16 [2, 8192, 640], P('rep', 'row', 'tp'), may hold values from -900 to 900
- gain_gradient: bfloat16 [2, 8, 3072], P('rep'), may hold values from -900 to 900
- master: float32 [4, 4, 2, 1556480], P('tp', 'row', 'rep'), may hold values from -5 to 5
- momentum: float32 [4, 4, 2, 1556480], P('tp', 'row', 'rep'), may hold values from -4 to 4
- variance: float32 [4, 4, 2, 1556480], P('tp', 'row', 'rep'), may hold values from 0.01 to 1
- entry_average: float32 [8, 640, 5632], P(None, 'row', 'tp'), may hold values from -5 to 5
- exit_average: float32 [8, 3072, 640], P(None, 'row', 'tp'), may hold values from -5 to 5
- embed_average: float32 [8192, 640], P('row', 'tp'), may hold values from -5 to 5
- gain_master: float32 [8, 3072], replicated, may hold values from -5 to 5
- gain_momentum: float32 [8, 3072], replicated, may hold values from -4 to 4
- gain_variance: float32 [8, 3072], replicated, may hold values from 0.01 to 1
Outputs:
- next_master: float32 [4, 4, 2, 1556480], P('tp', 'row', 'rep')
- next_momentum: float32 [4, 4, 2, 1556480], P('tp', 'row', 'rep')
- next_variance: float32 [4, 4, 2, 1556480], P('tp', 'row', 'rep')
- entry_weight: bfloat16 [8, 640, 5632], P(None, 'row', 'tp')
- exit_weight: bfloat16 [8, 3072, 640], P(None, 'row', 'tp')
- embed_weight: bfloat16 [8192, 640], P('row', 'tp')
- entry_averaged: float32 [8, 640, 5632], P(None, 'row', 'tp')
- exit_averaged: float32 [8, 3072, 640], P(None, 'row', 'tp')
- embed_averaged: float32 [8192, 640], P('row', 'tp')
- fresh_gain: float32 [8, 3072], replicated
- fresh_momentum: float32 [8, 3072], replicated
- fresh_variance: float32 [8, 3072], replicated
All inputs are finite; a program needn't handle non-finite values.
Results may differ from a plain program's by a relative error of at most 0.0028.
Values may be sent and summed in bfloat16 or wider, within the bound.
No kernel may reach another device: no remote copies, remote signals or barrier semaphores. Data moves between devices by JAX's collectives and lax.ppermute only.
A program may use at most 256 MiB of HBM per device.

v0:
```python
import math

import jax
import jax.numpy as jnp
from jax import lax
from jax.sharding import PartitionSpec as P

D = 640
VOCAB_ROWS = 8192
LAYERS = 8
IN_COLS = 5632
OUT_ROWS = 3072
NORM_LEN = 3072


beta_one = 0.9
beta_two = 0.95
learn_rate = 0.02
decay_rate = 0.1
epsilon = 1e-08
clip_level = 0.5
bias_one = 1.0 - 0.9**20
bias_two = 1.0 - 0.95**20
average_decay = 0.99


def clip_factor(square_sum):
    entries = LAYERS * (D * IN_COLS + OUT_ROWS * D + NORM_LEN) + VOCAB_ROWS * D
    return jnp.minimum(1.0, clip_level * math.sqrt(entries) / (jnp.sqrt(square_sum) + 1e-06))


def adam_update(gradient, momentum, variance, master, clip_scale):
    clipped = clip_scale * gradient
    moved_first = beta_one * momentum + (1.0 - beta_one) * clipped
    moved_second = beta_two * variance + (1.0 - beta_two) * clipped * clipped
    stepped = master * (1.0 - learn_rate * decay_rate) - learn_rate * (moved_first / bias_one) / (
        jnp.sqrt(moved_second / bias_two) + epsilon
    )
    return (stepped, moved_first, moved_second)


def strips_one(matrix_block, row_count, move_strips, sum_halves):
    layer_count, block_rows, block_cols = matrix_block.shape
    arrived = move_strips(matrix_block)
    arrived = arrived.reshape(layer_count, row_count, block_rows, block_cols // row_count).astype(
        jnp.float32
    )
    return sum_halves(arrived).reshape(-1)


def blocks_one(flat_part, layout, row_count, rep_count, copy_halves, move_blocks):
    layer_count, block_rows, block_cols = layout
    section = flat_part.reshape(
        layer_count, row_count, block_rows // rep_count, block_cols // row_count
    )
    section = copy_halves(section)
    section = move_blocks(section)
    return section.reshape(layer_count, block_rows, block_cols)


def shards(
    entry_gradient,
    exit_gradient,
    embed_gradient,
    gain_gradient,
    master,
    momentum,
    variance,
    entry_average,
    exit_average,
    embed_average,
    gain_master,
    gain_momentum,
    gain_variance,
):
    row_count = lax.axis_size("row")
    rep_count = lax.axis_size("rep")
    matrices = [entry_gradient[0], exit_gradient[0], embed_gradient[0][None]]
    layouts = [matrix_block.shape for matrix_block in matrices]
    flat_grad = jnp.concatenate(
        [
            strips_one(
                matrix_block,
                row_count,
                lambda moving: lax.all_to_all(
                    moving, "row", split_axis=2, concat_axis=1, tiled=True
                ),
                lambda moving: lax.psum_scatter(
                    moving.astype(jnp.bfloat16), "rep", scatter_dimension=2, tiled=True
                ).astype(jnp.float32),
            )
            for matrix_block in matrices
        ]
    )
    gain_local = gain_gradient[0].astype(jnp.float32)
    local_squares = jnp.sum(flat_grad * flat_grad)
    gain_total = lax.psum(gain_local.astype(jnp.bfloat16), "rep").astype(jnp.float32)
    square_sum = lax.psum(local_squares, ("rep", "row", "tp"))
    clip_scale = clip_factor(square_sum + jnp.sum(gain_total * gain_total))
    next_master, next_momentum, next_variance = adam_update(
        flat_grad, momentum.reshape(-1), variance.reshape(-1), master.reshape(-1), clip_scale
    )
    flat_weight = next_master.astype(jnp.bfloat16)
    weights = []
    offset = 0
    for layout in layouts:
        length = layout[0] * layout[1] * layout[2] // rep_count
        weights.append(
            blocks_one(
                flat_weight[offset : offset + length],
                layout,
                row_count,
                rep_count,
                lambda moving: lax.all_gather(moving, "rep", axis=2, tiled=True),
                lambda moving: lax.all_to_all(
                    moving, "row", split_axis=1, concat_axis=3, tiled=True
                ),
            )
        )
        offset = offset + length
    entry_weight = weights[0]
    exit_weight = weights[1]
    embed_weight = weights[2][0]
    entry_averaged = average_decay * entry_average + (1.0 - average_decay) * entry_weight.astype(
        jnp.float32
    )
    exit_averaged = average_decay * exit_average + (1.0 - average_decay) * exit_weight.astype(
        jnp.float32
    )
    embed_averaged = average_decay * embed_average + (1.0 - average_decay) * embed_weight.astype(
        jnp.float32
    )
    fresh_gain, fresh_momentum, fresh_variance = adam_update(
        gain_total, gain_momentum, gain_variance, gain_master, clip_scale
    )
    flat_shape = master.shape
    return (
        next_master.reshape(flat_shape),
        next_momentum.reshape(flat_shape),
        next_variance.reshape(flat_shape),
        entry_weight,
        exit_weight,
        embed_weight,
        entry_averaged,
        exit_averaged,
        embed_averaged,
        fresh_gain,
        fresh_momentum,
        fresh_variance,
    )


def solution(mesh):
    placed = (
        P("rep", None, "row", "tp"),
        P("rep", None, "row", "tp"),
        P("rep", "row", "tp"),
        P("rep", None, None),
        P("tp", "row", "rep", None),
        P("tp", "row", "rep", None),
        P("tp", "row", "rep", None),
        P(None, "row", "tp"),
        P(None, "row", "tp"),
        P("row", "tp"),
        P(),
        P(),
        P(),
    )
    return jax.shard_map(
        shards,
        mesh=mesh,
        in_specs=placed,
        out_specs=(
            P("tp", "row", "rep", None),
            P("tp", "row", "rep", None),
            P("tp", "row", "rep", None),
            P(None, "row", "tp"),
            P(None, "row", "tp"),
            P("row", "tp"),
            P(None, "row", "tp"),
            P(None, "row", "tp"),
            P("row", "tp"),
            P(),
            P(),
            P(),
        ),
        check_vma=False,
    )
```

profile of v0, /device:TPU:1, one launch (start us, length us, event | category | flops | bytes accessed | tf_op | source)
XLA Modules:
  0.0 613.5 jit_solution(723439849712705577)
XLA Ops:
  15.9 5.4 all-to-all-start.2
  25.2 13.0 %all-to-all-done.2 = bf16[4,2,40960]{2,1,0:T(2,128)(2,1)S(1)} async-done(((bf16[4,2,40960]{2,1,0:T(2,128)(2,1)}), bf16[4,2,40960]{2,1,0:T(2,128)(2,1)S(1)}, u32[]{:S(2)}, u32[]{:S(2)}) %all-to-all-start.2) | async-done | bytes 655392 | tf_op jit(solution)/shard_map/all_to_all | solution.py:85
  42.6 8.8 %copy.48 = bf16[1,8,160,1408]{2,1,3,0:T(8,128)(2,1)} copy(bf16[1,8,160,1408]{3,2,1,0:T(8,128)(2,1)} %param.13) | data formatting | bytes 7208960 | tf_op args[0]
  51.4 36.1 %all-to-all-done.1 = bf16[8,768,160]{1,0,2:T(8,128)(2,1)S(1)} async-done(((bf16[8,768,160]{1,0,2:T(8,128)(2,1)}), bf16[8,768,160]{1,0,2:T(8,128)(2,1)S(1)}, u32[]{:S(2)}, u32[]{:S(2)}) %all-to-all-start.1) | async-done | bytes 1966112 | tf_op jit(solution)/shard_map/all_to_all | solution.py:85
  87.5 5.2 all-to-all-start
  96.3 4.7 copy.51
  101.0 118.1 %all-to-all-done = bf16[8,160,1408]{1,0,2:T(8,128)(2,1)} async-done(((bf16[8,160,1408]{1,0,2:T(8,128)(2,1)}), bf16[8,160,1408]{1,0,2:T(8,128)(2,1)}, u32[]{:S(2)}, u32[]{:S(2)}) %all-to-all-start) | async-done | bytes 3604512 | tf_op jit(solution)/shard_map/all_to_all | solution.py:85
  219.1 8.3 %copy.49 = bf16[8,160,4,352]{3,1,2,0:T(8,128)(2,1)} copy(bf16[8,160,4,352]{1,0,3,2:T(8,128)(2,1)} %bitcast.1) | data formatting | bytes 7208960 | tf_op jit(solution)/shard_map/all_to_all | solution.py:85
  227.5 5.2 psum.15
  239.9 6.9 %reshape.154 = f32[491520]{0:T(1024)} reshape(bf16[8,4,384,40]{3,2,1,0:T(8,128)(2,1)} %reduce-scatter.6.cloned.1.call-done) | data formatting | bytes 2949120 | tf_op jit(solution)/shard_map/reshape | solution.py:48
  246.9 5.8 reshape.153
  260.7 7.5 %concatenate.25 = f32[1,1,1,491520]{3,2,1,0:T(1,128)} reshape(bf16[8,4,384,40]{3,2,1,0:T(8,128)(2,1)S(1)} %copy-done.1) | data formatting | bytes 2949120 | tf_op jit(solution)/shard_map/concatenate | solution.py:80
  268.2 37.1 %psum.14 = f32[]{:T(128)} all-reduce(f32[]{:T(128)} %multiply_reduce_fusion), channel_id=1, replica_groups=mesh['rep'=2,'row'=4,'tp'=4] {'rep','row','tp'}, use_global_device_ids=true, to_apply=%region_4.0 | all-reduce | flops 1 | bytes 8 | tf_op jit(solution)/shard_map/psum | solution.py:98
  306.7 9.3 %concatenate.24 = f32[1,1,1,901120]{3,2,1,0:T(1,128)} reshape(bf16[8,4,80,352]{3,2,1,0:T(8,128)(2,1)} %reduce-scatter.4.cloned.1.call-done) | data formatting | bytes 5406720 | tf_op jit(solution)/shard_map/concatenate | solution.py:80
  316.0 80.5 %divide_subtract_fusion = (f32[1,1,1,1556480]{3,2,1,0:T(1,128)}, f32[1,1,1,1556480]{3,2,1,0:T(1,128)}, f32[1,1,1,1556480]{3,2,1,0:T(1,128)}, f32[1,1,1,1556480]{...) fusion(f32[1,1,1,1556480]{3,2,1,0:T(1,128)} %param.17, f32[1,1,1,163840]{3,2,1,0:T(1,128)} %concatenate.26, ...), kind=kLoop, calls=%fused_computation.11 | loop fusion | flops 24903680 | bytes 62259204 | tf_op jit(solution)/shard_map/sub | solution.py:36
  396.5 8.6 %fusion.7 = bf16[1556480]{0:T(1024)(128)(2,1)S(1)} fusion(f32[1556480]{0:T(1024)} %bitcast.53, f32[1556480]{0:T(1024)} %bitcast.52, f32[1556480]{0:T(1024)} %bitcast.51, f32[1556480]{0:T(1024)S(1)} %bitcast.49, f32[]{:T(128)S(6)} %min_shard_map.3), kind=kLoop, calls=%fused_computation.14 | loop fusion | flops 18677760 | bytes 28016644 | tf_op jit(solution)/shard_map/convert_element_type | solution.py:103
  406.8 5.6 reshape.158
  431.1 6.4 %copy.57 = bf16[8,4,768,40]{2,3,0,1:T(8,128)(2,1)} copy(bf16[8,4,768,40]{3,2,1,0:T(8,128)(2,1)} %all-gather.5.cloned.1.call-done) | data formatting | bytes 3932160 | tf_op jit(solution)/shard_map/all_gather | solution.py:114
  452.0 38.7 %all-to-all-done.4 = bf16[8,4,768,40]{2,3,0,1:T(8,128)(2,1)S(1)} async-done(((bf16[8,4,768,40]{2,3,0,1:T(8,128)(2,1)}), bf16[8,4,768,40]{2,3,0,1:T(8,128)(2,1)S(1)}, u32[]{:S(2)}, u32[]{:S(2)}) %all-to-all-start.4) | async-done | bytes 1966112 | tf_op jit(solution)/shard_map/all_to_all | solution.py:115
  490.7 5.1 all-to-all-start.3
  504.1 78.8 %all-to-all-done.3 = bf16[8,4,160,352]{3,2,0,1:T(8,128)(2,1)} async-done(((bf16[8,4,160,352]{3,2,0,1:T(8,128)(2,1)}), bf16[8,4,160,352]{3,2,0,1:T(8,128)(2,1)}, u32[]{:S(2)}, u32[]{:S(2)}) %all-to-all-start.3) | async-done | bytes 3604512 | tf_op jit(solution)/shard_map/all_to_all | solution.py:115
  582.9 7.1 %copy.56 = bf16[8,1,160,4,352]{4,3,2,0,1:T(4,128)(2,1)} copy(bf16[8,1,160,4,352]{4,2,0,3,1:T(8,128)(2,1)} %bitcast.12) | data formatting | bytes 7208960 | tf_op jit(solution)/shard_map/all_to_all | solution.py:115
  590.0 7.6 %reshape.157 = bf16[8,160,1408]{2,1,0:T(8,128)(2,1)} reshape(bf16[8,1,160,4,352]{4,3,2,0,1:T(4,128)(2,1)} %copy.56) | data formatting | bytes 7208960 | tf_op jit(solution)/shard_map/reshape | solution.py:58
  597.6 8.3 %multiply_add_fusion = f32[8,160,1408]{2,1,0:T(8,128)} fusion(bf16[8,160,1408]{2,1,0:T(8,128)(2,1)} %reshape.157, f32[8,160,1408]{2,1,0:T(8,128)} %param.20), kind=kLoop, calls=%fused_computation.2 | loop fusion | flops 7208960 | bytes 18022400 | tf_op jit(solution)/shard_map/add | solution.py:124
  (80 shorter events, 79.8 us)
Async XLA Ops:
  15.9 22.3 %all-to-all-start.2 = ((bf16[4,2,40960]{2,1,0:T(2,128)(2,1)}), bf16[4,2,40960]{2,1,0:T(2,128)(2,1)S(1)}, u32[]{:S(2)}, u32[]{:S(2)}) async-start(bf16[4,2,40960]{2,1,0:T(2,128)(2,1)} %reshape.161), calls=%async_computation.4 | async-start | bytes 1310720 | tf_op jit(solution)/shard_map/all_to_all | solution.py:85
  39.0 48.5 %all-to-all-start.1 = ((bf16[8,768,160]{1,0,2:T(8,128)(2,1)}), bf16[8,768,160]{1,0,2:T(8,128)(2,1)S(1)}, u32[]{:S(2)}, u32[]{:S(2)}) async-start(bf16[8,768,160]{1,0,2:T(8,128)(2,1)} %bitcast.46), calls=%async_computation.2 | async-start | bytes 3932160 | tf_op jit(solution)/shard_map/all_to_all | solution.py:85
  87.5 131.6 %all-to-all-start = ((bf16[8,160,1408]{1,0,2:T(8,128)(2,1)}), bf16[8,160,1408]{1,0,2:T(8,128)(2,1)}, u32[]{:S(2)}, u32[]{:S(2)}) async-start(bf16[8,160,1408]{1,0,2:T(8,128)(2,1)} %bitcast.54), calls=%async_computation | async-start | bytes 11534336 | tf_op jit(solution)/shard_map/all_to_all | solution.py:85
  92.6 140.7 %reduce-scatter.8.cloned.1.call-start = ((), (), s32[]{:S(2)}) async-start(), calls=%async_computation.11 | async-start | bytes 983040 | tf_op jit(solution)/shard_map/reduce_scatter | solution.py:88
  96.3 143.7 %reduce-scatter.6.cloned.1.call-start = ((), (), s32[]{:S(2)}) async-start(), calls=%async_computation.10 | async-start | bytes 9437184 | tf_op jit(solution)/shard_map/reduce_scatter | solution.py:88
  101.0 145.9 %reduce-scatter.4.cloned.1.call-start = ((), (), s32[]{:S(2)}) async-start(), calls=%async_computation.9 | async-start | bytes 5898240 | tf_op jit(solution)/shard_map/reduce_scatter | solution.py:88
  219.1 8.3 %copy-start.12 = (bf16[1,8,3072]{2,1,0:T(8,128)(2,1)S(1)}, bf16[1,8,3072]{2,1,0:T(8,128)(2,1)}, u32[]{:S(2)}) copy-start(bf16[1,8,3072]{2,1,0:T(8,128)(2,1)} %param.16) | copy-start | bytes 147460
  227.4 203.7 %all-gather.5.cloned.1.call-start = ((), (), s32[]{:S(2)}) async-start(), calls=%async_computation.13 | async-start | bytes 9437184 | tf_op jit(solution)/shard_map/all_gather | solution.py:114
  255.3 5.4 copy-start.1
  255.5 3.0 copy-start
  306.7 89.8 %slice-start = ((s8[6225920]{0:T(1024)(128)(4,1)}), s8[2031616]{0:T(1024)(128)(4,1)S(1)}, s32[]{:S(2)}) async-start(s8[6225920]{0:T(1024)(128)(4,1)} %bitcast.48), calls=%async_computation.14 | async-start | bytes 4063232
  316.0 80.5 %slice-start.1 = ((s8[6225920]{0:T(1024)(128)(4,1)}), s8[4194304]{0:T(1024)(128)(4,1)S(1)}, s32[]{:S(2)}) async-start(s8[6225920]{0:T(1024)(128)(4,1)} %bitcast.48), calls=%async_computation.15 | async-start | bytes 8388608
  406.8 5.7 slice-start.2
  412.5 12.7 %slice-start.3 = ((bf16[1556480]{0:T(1024)(128)(2,1)}), bf16[901120]{0:T(1024)(128)(2,1)S(1)}, s32[]{:S(2)}) async-start(bf16[1556480]{0:T(1024)(128)(2,1)} %copy-done.2), calls=%async_computation.17 | async-start | bytes 3604480 | tf_op jit(solution)/shard_map/slice | solution.py:110
  421.1 21.0 %all-to-all-start.5 = ((bf16[1,4,2048,40]{2,3,0,1:T(8,128)(2,1)}), bf16[1,4,2048,40]{2,3,0,1:T(8,128)(2,1)S(1)}, u32[]{:S(2)}, u32[]{:S(2)}) async-start(bf16[1,4,2048,40]{2,3,0,1:T(8,128)(2,1)} %copy.59), calls=%async_computation.8 | async-start | bytes 1310720 | tf_op jit(solution)/shard_map/all_to_all | solution.py:115
  425.2 22.3 %all-gather.3.cloned.1.call-start = ((), (), s32[]{:S(2)}) async-start(), calls=%async_computation.12 | async-start | bytes 5898240 | tf_op jit(solution)/shard_map/all_gather | solution.py:114
  442.0 48.6 %all-to-all-start.4 = ((bf16[8,4,768,40]{2,3,0,1:T(8,128)(2,1)}), bf16[8,4,768,40]{2,3,0,1:T(8,128)(2,1)S(1)}, u32[]{:S(2)}, u32[]{:S(2)}) async-start(bf16[8,4,768,40]{2,3,0,1:T(8,128)(2,1)} %copy.57), calls=%async_computation.7 | async-start | bytes 3932160 | tf_op jit(solution)/shard_map/all_to_all | solution.py:115
  445.7 50.0 %copy-start.9 = (f32[8,3072]{1,0:T(8,128)S(1)}, f32[8,3072]{1,0:T(8,128)}, u32[]{:S(2)}) copy-start(f32[8,3072]{1,0:T(8,128)} %param.23) | copy-start | bytes 294916
  445.7 50.0 %copy-start.10 = (f32[8,3072]{1,0:T(8,128)S(1)}, f32[8,3072]{1,0:T(8,128)}, u32[]{:S(2)}) copy-start(f32[8,3072]{1,0:T(8,128)} %param.24) | copy-start | bytes 294916
  445.7 50.1 %copy-start.11 = (f32[8,3072]{1,0:T(8,128)S(1)}, f32[8,3072]{1,0:T(8,128)}, u32[]{:S(2)}) copy-start(f32[8,3072]{1,0:T(8,128)} %param.25) | copy-start | bytes 294916
  490.7 5.9 copy-start.4
  490.7 92.2 %all-to-all-start.3 = ((bf16[8,4,160,352]{3,2,0,1:T(8,128)(2,1)}), bf16[8,4,160,352]{3,2,0,1:T(8,128)(2,1)}, u32[]{:S(2)}, u32[]{:S(2)}) async-start(bf16[8,4,160,352]{3,2,0,1:T(8,128)(2,1)} %copy.55), calls=%async_computation.6 | async-start | bytes 7864320 | tf_op jit(solution)/shard_map/all_to_all | solution.py:115
  495.8 5.5 copy-start.6
  501.3 88.6 %copy-start.3 = (bf16[8,4,768,40]{2,3,1,0:T(8,128)(2,1)}, bf16[8,4,768,40]{2,3,1,0:T(8,128)(2,1)S(1)}, u32[]{:S(2)}) copy-start(bf16[8,4,768,40]{2,3,1,0:T(8,128)(2,1)S(1)} %copy.58) | copy-start | bytes 5898244
  (4 other events, 7.9 us)
Sparse Core Ops, SparseCore 0:
  96.4 10.4 reduce-scatter.7
  109.8 15.1 reduce-scatter.5
  227.5 12.3 reduce-scatter.3
  412.6 18.3 all-gather.4
  433.0 14.4 all-gather.2
where the time goes:
time: 623 us; the launch traced here: 614 us
  waiting for transfers between devices  294 us (47%)
  local copies, waits for them, and re-layouts  119 us (19%)
  other arithmetic  111 us (18%)
  blocking collectives  46.6 us (7%)
  starting transfers between devices  27.2 us (4%)
  between operations  15.7 us (3%)
    all_to_all x3, waiting for transfers between devices, shards(): lax.all_to_all(moving, 'row', split_axis=2, concat_axis=1, tiled=True)  167 us
    all_to_all x3, waiting for transfers between devices, shards(): lax.all_to_all(moving, 'row', split_axis=1, concat_axis=3, tiled=True)  122 us
    sub x2, other arithmetic, adam_update(): master * (1.0 - learn_rate * decay_rate)  81.2 us
    psum x1, blocking collectives, shards(): square_sum = lax.psum(local_squares, ('rep', 'row', 'tp'))  37.1 us
    unnamed x40, local copies, waits for them, and re-layouts  29.5 us
    concatenate x4, local copies, waits for them, and re-layouts, shards(): jnp.concatenate([strips_one(matrix_block, row_count, lambda moving: lax.a...  19.8 us
    reshape x3, local copies, waits for them, and re-layouts, strips_one(): return sum_halves(arrived).reshape(-1)  15.1 us
    all_to_all x3, starting transfers between devices, shards(): lax.all_to_all(moving, 'row', split_axis=2, concat_axis=1, tiled=True)  14.2 us
  transfers between devices with their start and end apart: 11, of which 8 were waited for; matrix products, arithmetic and copies ran while one was open for 11% of the time, Pallas kernels for 0%

commit v1 on v0

v1 whole, which is shorter than its diff:
```python
import math

import jax
import jax.numpy as jnp
from jax import lax
from jax.experimental import pallas as pl
from jax.experimental.pallas import tpu as pltpu
from jax.sharding import PartitionSpec as P

D = 640
VOCAB_ROWS = 8192
LAYERS = 8
IN_COLS = 5632
OUT_ROWS = 3072
NORM_LEN = 3072


beta_one = 0.9
beta_two = 0.95
learn_rate = 0.02
decay_rate = 0.1
epsilon = 1e-08
clip_level = 0.5
bias_one = 1.0 - 0.9**20
bias_two = 1.0 - 0.95**20
average_decay = 0.99


def clip_factor(square_sum):
    entries = LAYERS * (D * IN_COLS + OUT_ROWS * D + NORM_LEN) + VOCAB_ROWS * D
    return jnp.minimum(1.0, clip_level * math.sqrt(entries) / (jnp.sqrt(square_sum) + 1e-06))


def adam_update(gradient, momentum, variance, master, clip_scale):
    clipped = clip_scale * gradient
    moved_first = beta_one * momentum + (1.0 - beta_one) * clipped
    moved_second = beta_two * variance + (1.0 - beta_two) * clipped * clipped
    stepped = master * (1.0 - learn_rate * decay_rate) - learn_rate * (moved_first / bias_one) / (
        jnp.sqrt(moved_second / bias_two) + epsilon
    )
    return (stepped, moved_first, moved_second)


LANES = 128
TILE_ROWS = 640


def swap(moving, axis, distance):
    count = lax.axis_size(axis)
    return lax.ppermute(moving, axis, [(i, i ^ distance) for i in range(count)])


def all_sum(value, axis):
    count = lax.axis_size(axis)
    step = 1
    while step < count:
        if step * 2 < count:
            one = swap(value, axis, step)
            two = swap(value, axis, step * 2)
            three = swap(value, axis, step * 3)
            value = (value + one) + (two + three)
            step = step * 4
        else:
            value = value + swap(value, axis, step)
            step = step * 2
    return value


def half_sum(matrix_block):
    half = matrix_block.shape[1] // lax.axis_size("rep")
    mine = lax.axis_index("rep")
    kept = lax.dynamic_slice_in_dim(matrix_block, mine * half, half, 1)
    sent = lax.dynamic_slice_in_dim(matrix_block, (1 - mine) * half, half, 1)
    arrived = swap(sent, "rep", 1)
    return (kept.astype(jnp.float32) + arrived.astype(jnp.float32)).astype(jnp.bfloat16)


def both_halves(half):
    other = swap(half, "rep", 1)
    first = lax.axis_index("rep") == 0
    return jnp.concatenate(
        [jnp.where(first, half, other), jnp.where(first, other, half)], axis=1
    )


def to_owner(part, row_count):
    layer_count, half, block_cols = part.shape
    arrived = lax.all_to_all(part, "row", split_axis=2, concat_axis=1, tiled=True)
    return arrived.reshape(-1, LANES)


def to_holder(section, row_count):
    layer_count, row_count, half, width = section.shape
    block = lax.all_to_all(section, "row", split_axis=1, concat_axis=3, tiled=True)
    return block.reshape(layer_count, half, width * row_count)


def update_body(scale_ref, gradient_ref, momentum_ref, variance_ref, master_ref, *refs):
    master_out, momentum_out, variance_out, weight_out = refs[-4:]
    stepped, moved_first, moved_second = adam_update(
        gradient_ref[...].astype(jnp.float32),
        momentum_ref[...],
        variance_ref[...],
        master_ref[...],
        scale_ref[0, 0],
    )
    master_out[...] = stepped
    momentum_out[...] = moved_first
    variance_out[...] = moved_second
    weight_out[...] = stepped.astype(jnp.bfloat16)


def update_section(scale, gradient, momentum, variance, master, start, carried):
    rows = gradient.shape[0]
    tile = math.gcd(math.gcd(rows, start), TILE_ROWS)
    first = start // tile
    here = pl.BlockSpec((tile, LANES), lambda i: (i, 0))
    there = pl.BlockSpec((tile, LANES), lambda i: (i + first, 0))
    whole = jax.ShapeDtypeStruct(master.shape, jnp.float32)
    extra = [] if carried is None else list(carried)
    return pl.pallas_call(
        update_body,
        grid=(rows // tile,),
        in_specs=[pl.BlockSpec(memory_space=pltpu.SMEM), here, there, there, there]
        + [pl.BlockSpec(memory_space=pl.ANY) for _ in extra],
        out_specs=[there, there, there, here],
        out_shape=[whole, whole, whole, jax.ShapeDtypeStruct(gradient.shape, jnp.bfloat16)],
        input_output_aliases={5 + k: k for k in range(len(extra))},
        name="update",
    )(scale, gradient, momentum, variance, master, *extra)


def shards(
    entry_gradient,
    exit_gradient,
    embed_gradient,
    gain_gradient,
    master,
    momentum,
    variance,
    entry_average,
    exit_average,
    embed_average,
    gain_master,
    gain_momentum,
    gain_variance,
):
    row_count = lax.axis_size("row")
    matrices = [entry_gradient[0], exit_gradient[0], embed_gradient[0][None]]
    averages = [entry_average, exit_average, embed_average[None]]
    gain_local = gain_gradient[0]
    gain_total = gain_local.astype(jnp.float32) + swap(gain_local, "rep", 1).astype(jnp.float32)
    gain_total = gain_total.astype(jnp.bfloat16).astype(jnp.float32)
    sums = [half_sum(matrix_block) for matrix_block in matrices]
    local_squares = sum(jnp.sum(jnp.square(part.astype(jnp.float32))) for part in sums)
    local_squares = local_squares.reshape(1, 1)
    for axis in ("rep", "row", "tp"):
        local_squares = all_sum(local_squares, axis)
    clip_scale = clip_factor(local_squares + jnp.sum(gain_total * gain_total))

    flat = [array.reshape(-1, LANES) for array in (momentum, variance, master)]
    carried = None
    start = 0
    order = (0, 1, 2)
    starts = []
    for part in sums:
        starts.append(start)
        start = start + part.size // LANES
    weights = [None] * len(sums)
    averaged = [None] * len(sums)
    for k in order:
        part = sums[k]
        layer_count, half, block_cols = part.shape
        width = block_cols // row_count
        arrived = to_owner(part, row_count)
        *carried, weight = update_section(
            clip_scale, arrived, *flat, starts[k], carried
        )
        section = weight.reshape(layer_count, row_count, half, width)
        block = to_holder(section, row_count)
        weights[k] = both_halves(block)
        averaged[k] = average_decay * averages[k] + (1.0 - average_decay) * weights[k].astype(
            jnp.float32
        )
    fresh_gain, fresh_momentum, fresh_variance = adam_update(
        gain_total, gain_momentum, gain_variance, gain_master, clip_scale
    )
    next_master, next_momentum, next_variance = [array.reshape(master.shape) for array in carried]
    return (
        next_master,
        next_momentum,
        next_variance,
        weights[0],
        weights[1],
        weights[2][0],
        averaged[0],
        averaged[1],
        averaged[2][0],
        fresh_gain,
        fresh_momentum,
        fresh_variance,
    )


def solution(mesh):
    placed = (
        P("rep", None, "row", "tp"),
        P("rep", None, "row", "tp"),
        P("rep", "row", "tp"),
        P("rep", None, None),
        P("tp", "row", "rep", None),
        P("tp", "row", "rep", None),
        P("tp", "row", "rep", None),
        P(None, "row", "tp"),
        P(None, "row", "tp"),
        P("row", "tp"),
        P(),
        P(),
        P(),
    )
    return jax.shard_map(
        shards,
        mesh=mesh,
        in_specs=placed,
        out_specs=(
            P("tp", "row", "rep", None),
            P("tp", "row", "rep", None),
            P("tp", "row", "rep", None),
            P(None, "row", "tp"),
            P(None, "row", "tp"),
            P("row", "tp"),
            P(None, "row", "tp"),
            P(None, "row", "tp"),
            P("row", "tp"),
            P(),
            P(),
            P(),
        ),
        check_vma=False,
    )
```

time: 623 us -> 291 us (0.47); the launches traced: 614 us -> 290 us
  waiting for transfers between devices: 294 us -> 95.4 us
  other arithmetic: 111 us -> 25.9 us
  local copies, waits for them, and re-layouts: 119 us -> 57.6 us
  starting transfers between devices: 27.2 us -> 80 us
  blocking collectives: 46.6 us -> 0 us
  Pallas kernels: 0 us -> 23.2 us
  between operations: 15.7 us -> 7.74 us
    all_to_all x6, waiting for transfers between devices: 289 us -> 78.9 us  [the longest x3 55 us: to_holder(): lax.all_to_all(section, 'row', split_axis=1, concat_axis=3, tiled=True)]
    sub x2 -> x1, other arithmetic: 81.2 us -> 0.75 us  [adam_update(): master * (1.0 - learn_rate * decay_rate)]
    ppermute x0 -> x14, starting transfers between devices: none -> 53.4 us  [swap(): return lax.ppermute(moving, axis, [(i, i ^ distance) for i in range(count)])]
    psum x2 -> x0, blocking collectives: 42.3 us -> none  [the longest x1 37.1 us: shards(): square_sum = lax.psum(local_squares, ('rep', 'row', 'tp'))]
    unnamed x40 -> x28, local copies, waits for them, and re-layouts: 29.5 us -> 4.77 us
    pallas_call x0 -> x3, Pallas kernels: none -> 23.2 us  [update_section(): pl.pallas_call(update_body, grid=(rows // tile,), in_specs=[pl.BlockSpec(...]
    concatenate x4 -> x0, local copies, waits for them, and re-layouts: 19.8 us -> none  [shards(): jnp.concatenate([strips_one(matrix_block, row_count, lambda moving: lax.a...]
    ppermute x0 -> x14, waiting for transfers between devices: none -> 16.6 us  [swap(): return lax.ppermute(moving, axis, [(i, i ^ distance) for i in range(count)])]
  transfers between devices with their start and end apart: 11 -> 20, of which waited for: 8 -> 7; matrix products, arithmetic and copies ran while one was open for 11% -> 21% of each run, Pallas kernels for 0% -> 0%
where the time goes in v1:
time: 291 us; the launch traced here: 290 us
  waiting for transfers between devices  95.4 us (33%)
  starting transfers between devices  80 us (27%)
  local copies, waits for them, and re-layouts  57.6 us (20%)
  other arithmetic  25.9 us (9%)
  Pallas kernels  23.2 us (8%)
  between operations  7.74 us (3%)
    all_to_all x3, waiting for transfers between devices, to_holder(): lax.all_to_all(section, 'row', split_axis=1, concat_axis=3, tiled=True)  55 us
    ppermute x14, starting transfers between devices, swap(): return lax.ppermute(moving, axis, [(i, i ^ distance) for i in range(count)])  53.4 us
    all_to_all x3, waiting for transfers between devices, to_owner(): lax.all_to_all(part, 'row', split_axis=2, concat_axis=1, tiled=True)  23.8 us
    pallas_call x3, Pallas kernels, update_section(): pl.pallas_call(update_body, grid=(rows // tile,), in_specs=[pl.BlockSpec(...  23.2 us
    reshape x6, local copies, waits for them, and re-layouts, shards(): section = weight.reshape(layer_count, row_count, half, width)  17.3 us
    ppermute x14, waiting for transfers between devices, swap(): return lax.ppermute(moving, axis, [(i, i ^ distance) for i in range(count)])  16.6 us
    all_to_all x3, starting transfers between devices, to_owner(): lax.all_to_all(part, 'row', split_axis=2, concat_axis=1, tiled=True)  14.4 us
    reshape x3, local copies, waits for them, and re-layouts, to_owner(): return arrived.reshape(-1, LANES)  12.5 us
  transfers between devices with their start and end apart: 20, of which 7 were waited for; matrix products, arithmetic and copies ran while one was open for 21% of the time, Pallas kernels for 0%

profile of v1, /device:TPU:1, one launch (start us, length us, event | category | flops | bytes accessed | tf_op | source)
XLA Modules:
  0.0 289.9 jit_solution(11062776928902727693)
XLA Ops:
  12.5 6.1 %all-to-all-start = ((bf16[4,2,20480]{2,1,0:T(2,128)(2,1)}), bf16[4,2,20480]{2,1,0:T(2,128)(2,1)S(1)}, u32[]{:S(2)}, u32[]{:S(2)}) async-start(bf16[4,2,20480]{2,1,0:T(2,128)(2,1)} %reshape.111), calls=%async_computation | async-start | bytes 655360 | tf_op jit(solution)/shard_map/all_to_all | solution.py:88
  21.7 6.8 %all-to-all-done = bf16[4,2,20480]{2,1,0:T(2,128)(2,1)S(1)} async-done(((bf16[4,2,20480]{2,1,0:T(2,128)(2,1)}), bf16[4,2,20480]{2,1,0:T(2,128)(2,1)S(1)}, u32[]{:S(2)}, u32[]{:S(2)}) %all-to-all-start) | async-done | bytes 327712 | tf_op jit(solution)/shard_map/all_to_all | solution.py:88
  28.6 3.5 %all-to-all-start.1 = ((bf16[8,384,160]{1,0,2:T(8,128)(2,1)}), bf16[8,384,160]{1,0,2:T(8,128)(2,1)S(1)}, u32[]{:S(2)}, u32[]{:S(2)}) async-start(bf16[8,384,160]{1,0,2:T(8,128)(2,1)} %get-tuple-element.46), calls=%async_computation.1 | async-start | bytes 1966080 | tf_op jit(solution)/shard_map/all_to_all | solution.py:88
  32.1 3.6 %multiply_reduce_fusion = (f32[]{:T(128)}, bf16[8,80,1408]{2,1,0:T(8,128)(2,1)S(1)}) fusion(bf16[8,80,1408]{2,1,0:T(8,128)(2,1)} %collective-permute-done, bf16[1,8,160,1408]{3,2,1,0:T(8,128)(2,1)} %param.13, s32[]{:T(128)S(6)} %select_n.54), kind=kLoop, calls=%fused_computation.5 | loop fusion | flops 6307839 | bytes 5406728 | tf_op jit(solution)/shard_map/reduce_sum | solution.py:155
  39.0 17.0 %all-to-all-done.1 = bf16[8,384,160]{1,0,2:T(8,128)(2,1)S(1)} async-done(((bf16[8,384,160]{1,0,2:T(8,128)(2,1)}), bf16[8,384,160]{1,0,2:T(8,128)(2,1)S(1)}, u32[]{:S(2)}, u32[]{:S(2)}) %all-to-all-start.1) | async-done | bytes 983072 | tf_op jit(solution)/shard_map/all_to_all | solution.py:88
  56.0 4.8 %all-to-all-start.2 = ((bf16[8,80,1408]{1,0,2:T(8,128)(2,1)}), bf16[8,80,1408]{1,0,2:T(8,128)(2,1)}, u32[]{:S(2)}, u32[]{:S(2)}) async-start(bf16[8,80,1408]{1,0,2:T(8,128)(2,1)} %copy.79), calls=%async_computation.2 | async-start | bytes 5767168 | tf_op jit(solution)/shard_map/all_to_all | solution.py:88
  71.0 35.4 %collective-permute-start.4 = (f32[1,1]{1,0:T(1,128)}, f32[1,1]{1,0:T(1,128)}, u32[]{:S(2)}, u32[]{:S(2)}) collective-permute-start(f32[1,1]{1,0:T(1,128)} %add.99), channel_id=1, source_target_pairs={{0,4},{4,0},{8,12},{12,8},{1,5},{5,1},{9,13},{13,9},{2,6},{6,2},{1... | collective-permute-start | bytes 20 | tf_op jit(solution)/shard_map/ppermute | solution.py:50
  107.1 3.6 %collective-permute-start.6 = (f32[1,1]{1,0:T(1,128)}, f32[1,1]{1,0:T(1,128)}, u32[]{:S(2)}, u32[]{:S(2)}) collective-permute-start(f32[1,1]{1,0:T(1,128)} %add.99), channel_id=1, source_target_pairs={{0,12},{4,8},{8,4},{12,0},{1,13},{5,9},{9,5},{13,1},{2,14},{6,10},... | collective-permute-start | bytes 20 | tf_op jit(solution)/shard_map/ppermute | solution.py:50
  111.3 14.0 %collective-permute-done.5 = f32[1,1]{1,0:T(1,128)} collective-permute-done((f32[1,1]{1,0:T(1,128)}, f32[1,1]{1,0:T(1,128)}, u32[]{:S(2)}, u32[]{:S(2)}) %collective-permute-start.5) | collective-permute-done | bytes 36 | tf_op jit(solution)/shard_map/ppermute | solution.py:50
  138.5 5.8 %reshape.98.gradient_ref = bf16[3840,128]{1,0:T(8,128)(2,1)} reshape(bf16[8,4,384,40]{3,2,1,0:T(8,128)(2,1)S(1)} %bitcast.84) | data formatting | bytes 1966080 | tf_op jit(solution)/shard_map/reshape | solution.py:89
  144.2 3.6 %copy.80 = bf16[8,80,4,352]{3,1,2,0:T(8,128)(2,1)S(1)} copy(bf16[8,80,4,352]{1,0,3,2:T(8,128)(2,1)} %bitcast.13) | data formatting | bytes 3604480 | tf_op jit(solution)/shard_map/all_to_all | solution.py:88
  147.8 4.3 %reshape.99.gradient_ref = bf16[7040,128]{1,0:T(8,128)(2,1)} reshape(bf16[8,4,80,352]{3,2,1,0:T(8,128)(2,1)S(1)} %bitcast.85) | data formatting | bytes 3604480 | tf_op jit(solution)/shard_map/reshape | solution.py:89
  152.1 13.3 %update.3 = (f32[12160,128]{1,0:T(8,128)}, f32[12160,128]{1,0:T(8,128)}, f32[12160,128]{1,0:T(8,128)}, bf16[7040,128]{1,0:T(8,128)(2,1)}) custom-call(f32[1,1]{1,0:T(1,128)} %min.3.scale_ref, bf16[7040,128]{1,0:T(8,128)(2,1)} %reshape.99.gradient_ref, f32[12160,128]{1,0:T(8,128)} %bitcast.72, f32[12160,128]{1,0:T(8,128)} %bitcast.75, f32[12160,128]{1,0:T(8,128)} %bitcast.78), custom_call_target="tpu_custom_call" | custom-call | tf_op jit(solution)/shard_map/update/pallas_call | solution.py:121
  165.4 7.1 %update.4 = (f32[12160,128]{1,0:T(8,128)}, f32[12160,128]{1,0:T(8,128)}, f32[12160,128]{1,0:T(8,128)}, bf16[3840,128]{1,0:T(8,128)(2,1)}) custom-call(f32[1,1]{1,0:T(1,128)} %min.3.scale_ref, bf16[3840,128]{1,0:T(8,128)(2,1)} %reshape.98.gradient_ref, f32[12160,128]{1,0:T(8,128)} %bitcast.73, ...), custom_call_target="tpu_custom_call", output_to_operand_aliasing={{0}: (5, {}), {1}: (6, {}), {2}: (7, {})} | custom-call | tf_op jit(solution)/shard_map/update/pallas_call | solution.py:121
  179.0 4.1 %all-to-all-start.5 = ((bf16[1,4,1024,40]{2,3,0,1:T(8,128)(2,1)}), bf16[1,4,1024,40]{2,3,0,1:T(8,128)(2,1)}, u32[]{:S(2)}, u32[]{:S(2)}) async-start(bf16[1,4,1024,40]{2,3,0,1:T(8,128)(2,1)} %copy.85), calls=%async_computation.5 | async-start | bytes 655360 | tf_op jit(solution)/shard_map/all_to_all | solution.py:94
  183.1 6.0 %reshape.105 = bf16[8,4,384,40]{3,2,1,0:T(8,128)(2,1)S(1)} reshape(bf16[3840,128]{1,0:T(8,128)(2,1)} %get-tuple-element.34) | data formatting | bytes 1966080 | tf_op jit(solution)/shard_map/reshape | solution.py:179
  191.3 4.5 %all-to-all-start.4 = ((bf16[8,4,384,40]{2,3,0,1:T(8,128)(2,1)}), bf16[8,4,384,40]{2,3,0,1:T(8,128)(2,1)S(1)}, u32[]{:S(2)}, u32[]{:S(2)}) async-start(bf16[8,4,384,40]{2,3,0,1:T(8,128)(2,1)} %copy.83), calls=%async_computation.4 | async-start | bytes 1966080 | tf_op jit(solution)/shard_map/all_to_all | solution.py:94
  195.8 3.9 %reshape.103 = bf16[8,4,80,352]{3,2,1,0:T(8,128)(2,1)S(1)} reshape(bf16[7040,128]{1,0:T(8,128)(2,1)} %get-tuple-element.33) | data formatting | bytes 3604480 | tf_op jit(solution)/shard_map/reshape | solution.py:179
  201.2 16.0 %all-to-all-done.4 = bf16[8,4,384,40]{2,3,0,1:T(8,128)(2,1)S(1)} async-done(((bf16[8,4,384,40]{2,3,0,1:T(8,128)(2,1)}), bf16[8,4,384,40]{2,3,0,1:T(8,128)(2,1)S(1)}, u32[]{:S(2)}, u32[]{:S(2)}) %all-to-all-start.4) | async-done | bytes 983072 | tf_op jit(solution)/shard_map/all_to_all | solution.py:94
  217.2 3.6 %all-to-all-start.3 = ((bf16[8,4,80,352]{3,2,0,1:T(8,128)(2,1)}), bf16[8,4,80,352]{3,2,0,1:T(8,128)(2,1)S(1)}, u32[]{:S(2)}, u32[]{:S(2)}) async-start(bf16[8,4,80,352]{3,2,0,1:T(8,128)(2,1)} %copy.81), calls=%async_computation.3 | async-start | bytes 3932160 | tf_op jit(solution)/shard_map/all_to_all | solution.py:94
  220.8 4.0 %collective-permute-start.13 = (bf16[1,1024,160]{1,2,0:T(8,128)(2,1)}, bf16[1,1024,160]{1,2,0:T(8,128)(2,1)}, u32[]{:S(2)}, u32[]{:S(2)}) collective-permute-start(bf16[1,1024,160]{1,2,0:T(8,128)(2,1)} %bitcast.27), channel_id=1, source_target_pairs={{0,16},{16,0},{1,17},{17,1},{2,18},{18,2},{3,19},{19,3},{4,20},{20... | collective-permute-start | bytes 983048 | tf_op jit(solution)/shard_map/ppermute | solution.py:50
  226.6 39.1 %all-to-all-done.3 = bf16[8,4,80,352]{3,2,0,1:T(8,128)(2,1)S(1)} async-done(((bf16[8,4,80,352]{3,2,0,1:T(8,128)(2,1)}), bf16[8,4,80,352]{3,2,0,1:T(8,128)(2,1)S(1)}, u32[]{:S(2)}, u32[]{:S(2)}) %all-to-all-start.3) | async-done | bytes 1802272 | tf_op jit(solution)/shard_map/all_to_all | solution.py:94
  279.2 3.8 %multiply_add_fusion.1 = (f32[8,768,160]{1,2,0:T(8,128)}, bf16[8,768,160]{1,2,0:T(8,128)(2,1)}) fusion(f32[8,768,160]{1,2,0:T(8,128)S(1)} %copy-done.2, bf16[8,384,160]{1,2,0:T(8,128)(2,1)S(1)} %get-tuple-element.52, bf16[8,384,160]{1,2,0:T(8,128)(2,1)S(1)} %get-tuple-element.51), kind=kLoop, calls=%fused_computation.1 | loop fusion | flops 7864320 | bytes 11796480 | tf_op jit(solution)/shard_map/add | solution.py:182
  284.9 5.0 %multiply_add_fusion = (f32[8,160,1408]{2,1,0:T(8,128)}, bf16[8,160,1408]{2,1,0:T(8,128)(2,1)}) fusion(f32[8,160,1408]{2,1,0:T(8,128)S(1)} %bitcast.88, bf16[8,80,1408]{2,1,0:T(8,128)(2,1)S(1)} %get-tuple-element.50, bf16[8,80,1408]{2,1,0:T(8,128)(2,1)S(1)} %get-tuple-element.49), kind=kLoop, calls=%fused_computation | loop fusion | flops 14417920 | bytes 21626880 | tf_op jit(solution)/shard_map/add | solution.py:182
  (82 shorter events, 63.5 us)
Async XLA Ops:
  3.7 14.8 %collective-permute-start.1 = (bf16[8,384,160]{1,0,2:T(8,128)(2,1)}, bf16[8,384,160]{1,0,2:T(8,128)(2,1)}, u32[]{:S(2)}, u32[]{:S(2)}) collective-permute-start(bf16[8,384,160]{1,0,2:T(8,128)(2,1)} %bitcast.70), channel_id=1, source_target_pairs={{0,16},{16,0},{1,17},{17,1},{2,18},{18,2},{3,19},{19,3},{4,20},{20... | collective-permute-start | bytes 2949128 | tf_op jit(solution)/shard_map/ppermute | solution.py:50
  3.7 3.4 %collective-permute-start.2 = (bf16[1,1024,160]{1,2,0:T(8,128)(2,1)S(1)}, bf16[1,1024,160]{1,2,0:T(8,128)(2,1)S(1)}, u32[]{:S(2)}, u32[]{:S(2)}) collective-permute-start(bf16[1,1024,160]{1,2,0:T(8,128)(2,1)S(1)} %constant_dynamic-slice_fusion), channel_id=1, source_target_pairs={{0,16},{16,0},{1,17},{17,1},{2,18},{18,2},{3,19},{19,3},{4,20},{20... | collective-permute-start | bytes 983048 | tf_op jit(solution)/shard_map/ppermute | solution.py:50
  7.1 25.0 %collective-permute-start = (bf16[8,80,1408]{2,1,0:T(8,128)(2,1)}, bf16[8,80,1408]{2,1,0:T(8,128)(2,1)}, u32[]{:S(2)}, u32[]{:S(2)}) collective-permute-start(bf16[8,80,1408]{2,1,0:T(8,128)(2,1)} %dynamic-slice_bitcast_fusion), channel_id=1, source_target_pairs={{0,16},{16,0},{1,17},{17,1},{2,18},{18,2},{3,19},{19,3},{4,20},{20... | collective-permute-start | bytes 5406728 | tf_op jit(solution)/shard_map/ppermute | solution.py:50
  12.5 16.1 %all-to-all-start = ((bf16[4,2,20480]{2,1,0:T(2,128)(2,1)}), bf16[4,2,20480]{2,1,0:T(2,128)(2,1)S(1)}, u32[]{:S(2)}, u32[]{:S(2)}) async-start(bf16[4,2,20480]{2,1,0:T(2,128)(2,1)} %reshape.111), calls=%async_computation | async-start | bytes 655360 | tf_op jit(solution)/shard_map/all_to_all | solution.py:88
  28.6 27.4 %all-to-all-start.1 = ((bf16[8,384,160]{1,0,2:T(8,128)(2,1)}), bf16[8,384,160]{1,0,2:T(8,128)(2,1)S(1)}, u32[]{:S(2)}, u32[]{:S(2)}) async-start(bf16[8,384,160]{1,0,2:T(8,128)(2,1)} %get-tuple-element.46), calls=%async_computation.1 | async-start | bytes 1966080 | tf_op jit(solution)/shard_map/all_to_all | solution.py:88
  39.0 21.8 %copy-start.6 = (bf16[1,8,3072]{2,1,0:T(8,128)(2,1)S(1)}, bf16[1,8,3072]{2,1,0:T(8,128)(2,1)}, u32[]{:S(2)}) copy-start(bf16[1,8,3072]{2,1,0:T(8,128)(2,1)} %param.16) | copy-start | bytes 147460
  56.0 88.3 %all-to-all-start.2 = ((bf16[8,80,1408]{1,0,2:T(8,128)(2,1)}), bf16[8,80,1408]{1,0,2:T(8,128)(2,1)}, u32[]{:S(2)}, u32[]{:S(2)}) async-start(bf16[8,80,1408]{1,0,2:T(8,128)(2,1)} %copy.79), calls=%async_computation.2 | async-start | bytes 5767168 | tf_op jit(solution)/shard_map/all_to_all | solution.py:88
  60.8 2.3 collective-permute-start.10
  69.0 1.4 collective-permute-start.3
  71.0 39.7 %collective-permute-start.4 = (f32[1,1]{1,0:T(1,128)}, f32[1,1]{1,0:T(1,128)}, u32[]{:S(2)}, u32[]{:S(2)}) collective-permute-start(f32[1,1]{1,0:T(1,128)} %add.99), channel_id=1, source_target_pairs={{0,4},{4,0},{8,12},{12,8},{1,5},{5,1},{9,13},{13,9},{2,6},{6,2},{1... | collective-permute-start | bytes 20 | tf_op jit(solution)/shard_map/ppermute | solution.py:50
  106.4 18.9 %collective-permute-start.5 = (f32[1,1]{1,0:T(1,128)}, f32[1,1]{1,0:T(1,128)}, u32[]{:S(2)}, u32[]{:S(2)}) collective-permute-start(f32[1,1]{1,0:T(1,128)} %add.99), channel_id=1, source_target_pairs={{0,8},{4,12},{8,0},{12,4},{1,9},{5,13},{9,1},{13,5},{2,10},{6,14},... | collective-permute-start | bytes 20 | tf_op jit(solution)/shard_map/ppermute | solution.py:50
  107.1 18.2 %collective-permute-start.6 = (f32[1,1]{1,0:T(1,128)}, f32[1,1]{1,0:T(1,128)}, u32[]{:S(2)}, u32[]{:S(2)}) collective-permute-start(f32[1,1]{1,0:T(1,128)} %add.99), channel_id=1, source_target_pairs={{0,12},{4,8},{8,4},{12,0},{1,13},{5,9},{9,5},{13,1},{2,14},{6,10},... | collective-permute-start | bytes 20 | tf_op jit(solution)/shard_map/ppermute | solution.py:50
  126.4 4.9 %collective-permute-start.7 = (f32[1,1]{1,0:T(1,128)}, f32[1,1]{1,0:T(1,128)}, u32[]{:S(2)}, u32[]{:S(2)}) collective-permute-start(f32[1,1]{1,0:T(1,128)} %add.102), channel_id=1, source_target_pairs={{0,1},{1,0},{2,3},{3,2},{4,5},{5,4},{6,7},{7,6},{8,9},{9,8},{10,11... | collective-permute-start | bytes 20 | tf_op jit(solution)/shard_map/ppermute | solution.py:50
  128.4 3.5 %collective-permute-start.8 = (f32[1,1]{1,0:T(1,128)}, f32[1,1]{1,0:T(1,128)}, u32[]{:S(2)}, u32[]{:S(2)}) collective-permute-start(f32[1,1]{1,0:T(1,128)} %add.102), channel_id=1, source_target_pairs={{0,2},{1,3},{2,0},{3,1},{4,6},{5,7},{6,4},{7,5},{8,10},{9,11},{10,... | collective-permute-start | bytes 20 | tf_op jit(solution)/shard_map/ppermute | solution.py:50
  130.4 3.3 %collective-permute-start.9 = (f32[1,1]{1,0:T(1,128)}, f32[1,1]{1,0:T(1,128)}, u32[]{:S(2)}, u32[]{:S(2)}) collective-permute-start(f32[1,1]{1,0:T(1,128)} %add.102), channel_id=1, source_target_pairs={{0,3},{1,2},{2,1},{3,0},{4,7},{5,6},{6,5},{7,4},{8,11},{9,10},{10,... | collective-permute-start | bytes 20 | tf_op jit(solution)/shard_map/ppermute | solution.py:50
  179.0 12.3 %all-to-all-start.5 = ((bf16[1,4,1024,40]{2,3,0,1:T(8,128)(2,1)}), bf16[1,4,1024,40]{2,3,0,1:T(8,128)(2,1)}, u32[]{:S(2)}, u32[]{:S(2)}) async-start(bf16[1,4,1024,40]{2,3,0,1:T(8,128)(2,1)} %copy.85), calls=%async_computation.5 | async-start | bytes 655360 | tf_op jit(solution)/shard_map/all_to_all | solution.py:94
  191.3 25.8 %all-to-all-start.4 = ((bf16[8,4,384,40]{2,3,0,1:T(8,128)(2,1)}), bf16[8,4,384,40]{2,3,0,1:T(8,128)(2,1)S(1)}, u32[]{:S(2)}, u32[]{:S(2)}) async-start(bf16[8,4,384,40]{2,3,0,1:T(8,128)(2,1)} %copy.83), calls=%async_computation.4 | async-start | bytes 1966080 | tf_op jit(solution)/shard_map/all_to_all | solution.py:94
  201.2 23.6 %copy-start.7 = (f32[8,3072]{1,0:T(8,128)S(1)}, f32[8,3072]{1,0:T(8,128)}, u32[]{:S(2)}) copy-start(f32[8,3072]{1,0:T(8,128)} %param.23) | copy-start | bytes 294916
  201.2 23.6 %copy-start.8 = (f32[8,3072]{1,0:T(8,128)S(1)}, f32[8,3072]{1,0:T(8,128)}, u32[]{:S(2)}) copy-start(f32[8,3072]{1,0:T(8,128)} %param.24) | copy-start | bytes 294916
  201.2 23.6 %copy-start.9 = (f32[8,3072]{1,0:T(8,128)S(1)}, f32[8,3072]{1,0:T(8,128)}, u32[]{:S(2)}) copy-start(f32[8,3072]{1,0:T(8,128)} %param.25) | copy-start | bytes 294916
  217.2 48.5 %all-to-all-start.3 = ((bf16[8,4,80,352]{3,2,0,1:T(8,128)(2,1)}), bf16[8,4,80,352]{3,2,0,1:T(8,128)(2,1)S(1)}, u32[]{:S(2)}, u32[]{:S(2)}) async-start(bf16[8,4,80,352]{3,2,0,1:T(8,128)(2,1)} %copy.81), calls=%async_computation.3 | async-start | bytes 3932160 | tf_op jit(solution)/shard_map/all_to_all | solution.py:94
  220.8 53.0 %collective-permute-start.13 = (bf16[1,1024,160]{1,2,0:T(8,128)(2,1)}, bf16[1,1024,160]{1,2,0:T(8,128)(2,1)}, u32[]{:S(2)}, u32[]{:S(2)}) collective-permute-start(bf16[1,1024,160]{1,2,0:T(8,128)(2,1)} %bitcast.27), channel_id=1, source_target_pairs={{0,16},{16,0},{1,17},{17,1},{2,18},{18,2},{3,19},{19,3},{4,20},{20... | collective-permute-start | bytes 983048 | tf_op jit(solution)/shard_map/ppermute | solution.py:50
  226.5 50.5 %collective-permute-start.12 = (bf16[8,384,160]{1,2,0:T(8,128)(2,1)}, bf16[8,384,160]{1,2,0:T(8,128)(2,1)}, u32[]{:S(2)}, u32[]{:S(2)}) collective-permute-start(bf16[8,384,160]{1,2,0:T(8,128)(2,1)} %bitcast.22), channel_id=1, source_target_pairs={{0,16},{16,0},{1,17},{17,1},{2,18},{18,2},{3,19},{19,3},{4,20},{20... | collective-permute-start | bytes 2949128 | tf_op jit(solution)/shard_map/ppermute | solution.py:50
  272.4 10.6 %collective-permute-start.11 = (bf16[8,80,1408]{2,1,0:T(8,128)(2,1)}, bf16[8,80,1408]{2,1,0:T(8,128)(2,1)S(1)}, u32[]{:S(2)}, u32[]{:S(2)}) collective-permute-start(bf16[8,80,1408]{2,1,0:T(8,128)(2,1)} %reshape.104), channel_id=1, source_target_pairs={{0,16},{16,0},{1,17},{17,1},{2,18},{18,2},{3,19},{19,3},{4,20},{20... | collective-permute-start | bytes 5406728 | tf_op jit(solution)/shard_map/ppermute | solution.py:50
  (8 other events, 32.7 us)

commit v2 on v1

--- a/solution.py
+++ b/solution.py
@@ -66,6 +66,10 @@
     return value
 
 
+def after(value, *earlier):
+    return lax.optimization_barrier((value, *earlier))[0]
+
+
 def half_sum(matrix_block):
     half = matrix_block.shape[1] // lax.axis_size("rep")
     mine = lax.axis_index("rep")
@@ -85,7 +89,11 @@
 
 def to_owner(part, row_count):
     layer_count, half, block_cols = part.shape
-    arrived = lax.all_to_all(part, "row", split_axis=2, concat_axis=1, tiled=True)
+    if half % LANES == 0:
+        arrived = lax.all_to_all(part, "row", split_axis=2, concat_axis=1, tiled=True)
+    else:
+        pieces = part.reshape(layer_count, half, row_count, -1).transpose(0, 2, 1, 3)
+        arrived = lax.all_to_all(pieces, "row", split_axis=1, concat_axis=1, tiled=True)
     return arrived.reshape(-1, LANES)
 
 
@@ -154,34 +162,33 @@
     sums = [half_sum(matrix_block) for matrix_block in matrices]
     local_squares = sum(jnp.sum(jnp.square(part.astype(jnp.float32))) for part in sums)
     local_squares = local_squares.reshape(1, 1)
-    for axis in ("rep", "row", "tp"):
+    for axis in ("rep", "tp", "row"):
         local_squares = all_sum(local_squares, axis)
     clip_scale = clip_factor(local_squares + jnp.sum(gain_total * gain_total))
 
     flat = [array.reshape(-1, LANES) for array in (momentum, variance, master)]
+    starts = [0, sums[0].size // LANES, (sums[0].size + sums[1].size) // LANES]
+    arrived = [None] * 3
+    arrived[2] = to_owner(sums[2], row_count)
+    arrived[1] = to_owner(after(sums[1], arrived[2]), row_count)
+    arrived[0] = to_owner(after(sums[0], arrived[1], clip_scale), row_count)
     carried = None
-    start = 0
-    order = (0, 1, 2)
-    starts = []
-    for part in sums:
-        starts.append(start)
-        start = start + part.size // LANES
-    weights = [None] * len(sums)
-    averaged = [None] * len(sums)
-    for k in order:
-        part = sums[k]
-        layer_count, half, block_cols = part.shape
-        width = block_cols // row_count
-        arrived = to_owner(part, row_count)
+    updated = [None] * 3
+    for k in (2, 1, 0):
+        layer_count, half, block_cols = sums[k].shape
         *carried, weight = update_section(
-            clip_scale, arrived, *flat, starts[k], carried
+            clip_scale, arrived[k], *flat, starts[k], carried
         )
-        section = weight.reshape(layer_count, row_count, half, width)
-        block = to_holder(section, row_count)
-        weights[k] = both_halves(block)
-        averaged[k] = average_decay * averages[k] + (1.0 - average_decay) * weights[k].astype(
-            jnp.float32
-        )
+        updated[k] = weight.reshape(layer_count, row_count, half, block_cols // row_count)
+    blocks = [None] * 3
+    blocks[1] = to_holder(after(updated[1], arrived[0]), row_count)
+    blocks[0] = to_holder(after(updated[0], blocks[1]), row_count)
+    blocks[2] = to_holder(after(updated[2], blocks[0]), row_count)
+    weights = [both_halves(block) for block in blocks]
+    averaged = [
+        average_decay * average + (1.0 - average_decay) * weight.astype(jnp.float32)
+        for average, weight in zip(averages, weights)
+    ]
     fresh_gain, fresh_momentum, fresh_variance = adam_update(
         gain_total, gain_momentum, gain_variance, gain_master, clip_scale
     )

time: 291 us -> 258 us (0.89)
  starting transfers between devices: 80 us -> 46.1 us
  waiting for transfers between devices: 95.4 us -> 90.6 us
  other arithmetic: 25.9 us -> 29 us
    ppermute x14, starting transfers between devices: 53.4 us -> 21.5 us  [swap(): return lax.ppermute(moving, axis, [(i, i ^ distance) for i in range(count)])]
    all_to_all x0 -> x1, waiting for transfers between devices: none -> 29.1 us  [to_owner(): lax.all_to_all(pieces, 'row', split_axis=1, concat_axis=1, tiled=True)]
    all_to_all x3 -> x2, waiting for transfers between devices: 23.8 us -> 5.11 us  [to_owner(): lax.all_to_all(part, 'row', split_axis=2, concat_axis=1, tiled=True)]
    ppermute x14, waiting for transfers between devices: 16.6 us -> 4.25 us  [swap(): return lax.ppermute(moving, axis, [(i, i ^ distance) for i in range(count)])]
    all_to_all x3 -> x2, starting transfers between devices: 14.4 us -> 9.29 us  [to_owner(): lax.all_to_all(part, 'row', split_axis=2, concat_axis=1, tiled=True)]
    optimization_barrier x0 -> x3, local copies, waits for them, and re-layouts: none -> 4.76 us  [after(): return lax.optimization_barrier((value, *earlier))[0]]
    all_to_all x0 -> x1, starting transfers between devices: none -> 4.43 us  [to_owner(): lax.all_to_all(pieces, 'row', split_axis=1, concat_axis=1, tiled=True)]
    all_to_all x3 -> x2, local copies, waits for them, and re-layouts: 6.99 us -> 3.42 us  [to_owner(): lax.all_to_all(part, 'row', split_axis=2, concat_axis=1, tiled=True)]
  transfers between devices with their start and end apart: 20 -> 20, of which waited for: 7 -> 8; matrix products, arithmetic and copies ran while one was open for 21% -> 20% of each run, Pallas kernels for 0% -> 9%
where the time goes in v2:
time: 258 us; the launch traced here: 257 us
  waiting for transfers between devices  90.6 us (35%)
  local copies, waits for them, and re-layouts  60.2 us (23%)
  starting transfers between devices  46.1 us (18%)
  other arithmetic  29 us (11%)
  Pallas kernels  23.2 us (9%)
  between operations  7.82 us (3%)
    all_to_all x3, waiting for transfers between devices, to_holder(): lax.all_to_all(section, 'row', split_axis=1, concat_axis=3, tiled=True)  52.1 us
    all_to_all x1, waiting for transfers between devices, to_owner(): lax.all_to_all(pieces, 'row', split_axis=1, concat_axis=1, tiled=True)  29.1 us
    pallas_call x3, Pallas kernels, update_section(): pl.pallas_call(update_body, grid=(rows // tile,), in_specs=[pl.BlockSpec(...  23.2 us
    ppermute x14, starting transfers between devices, swap(): return lax.ppermute(moving, axis, [(i, i ^ distance) for i in range(count)])  21.5 us
    reshape x3, local copies, waits for them, and re-layouts, to_owner(): return arrived.reshape(-1, LANES)  13.8 us
    add x3, other arithmetic, shards(): average_decay * average + (1.0 - average_decay) * weight.astype(jnp.float32)  12.1 us
    reshape x3, local copies, waits for them, and re-layouts, shards(): weight.reshape(layer_count, row_count, half, block_cols // row_count)  11.4 us
    all_to_all x3, starting transfers between devices, to_holder(): lax.all_to_all(section, 'row', split_axis=1, concat_axis=3, tiled=True)  10.9 us
  transfers between devices with their start and end apart: 20, of which 8 were waited for; matrix products, arithmetic and copies ran while one was open for 20% of the time, Pallas kernels for 9%

profile of v2, /device:TPU:1, one launch (start us, length us, event | category | flops | bytes accessed | tf_op | source)
XLA Modules:
  0.0 256.9 jit_solution(17315559082982635497)
XLA Ops:
  10.5 5.6 %all-to-all-start = ((bf16[4,2,20480]{2,1,0:T(2,128)(2,1)}), bf16[4,2,20480]{2,1,0:T(2,128)(2,1)S(1)}, u32[]{:S(2)}, u32[]{:S(2)}) async-start(bf16[4,2,20480]{2,1,0:T(2,128)(2,1)} %reshape.114), calls=%async_computation | async-start | bytes 655360 | tf_op jit(solution)/shard_map/all_to_all | solution.py:93
  19.7 5.1 %all-to-all-done = bf16[4,2,20480]{2,1,0:T(2,128)(2,1)S(1)} async-done(((bf16[4,2,20480]{2,1,0:T(2,128)(2,1)}), bf16[4,2,20480]{2,1,0:T(2,128)(2,1)S(1)}, u32[]{:S(2)}, u32[]{:S(2)}) %all-to-all-start) | async-done | bytes 327712 | tf_op jit(solution)/shard_map/all_to_all | solution.py:93
  30.1 3.7 %all-to-all-start.1 = ((bf16[8,384,160]{1,0,2:T(8,128)(2,1)}), bf16[8,384,160]{1,0,2:T(8,128)(2,1)S(1)}, u32[]{:S(2)}, u32[]{:S(2)}) async-start(bf16[8,384,160]{1,0,2:T(8,128)(2,1)} %get-tuple-element.29), calls=%async_computation.1 | async-start | bytes 1966080 | tf_op jit(solution)/shard_map/all_to_all | solution.py:93
  38.0 4.7 %multiply_reduce_fusion = (f32[]{:T(128)}, bf16[8,80,1408]{2,1,0:T(8,128)(2,1)}) fusion(bf16[8,80,1408]{2,1,0:T(8,128)(2,1)} %collective-permute-done, bf16[1,8,160,1408]{3,2,1,0:T(8,128)(2,1)} %param.13, s32[]{:T(128)S(6)} %select_n.54), kind=kLoop, calls=%fused_computation.5 | loop fusion | flops 6307839 | bytes 5406728 | tf_op jit(solution)/shard_map/reduce_sum | solution.py:163
  54.9 3.3 %collective-permute-start.8 = (f32[1,1]{1,0:T(1,128)}, f32[1,1]{1,0:T(1,128)}, u32[]{:S(2)}, u32[]{:S(2)}) collective-permute-start(f32[1,1]{1,0:T(1,128)} %add.102), channel_id=1, source_target_pairs={{0,8},{4,12},{8,0},{12,4},{1,9},{5,13},{9,1},{13,5},{2,10},{6,14},... | collective-permute-start | bytes 20 | tf_op jit(solution)/shard_map/ppermute | solution.py:50
  68.9 5.8 %reshape.97.gradient_ref = bf16[3840,128]{1,0:T(8,128)(2,1)} reshape(bf16[8,4,384,40]{3,2,1,0:T(8,128)(2,1)S(1)} %bitcast.83) | data formatting | bytes 1966080 | tf_op jit(solution)/shard_map/reshape | solution.py:97
  74.7 4.3 %reshape.98 = bf16[8,80,4,352]{3,2,1,0:T(4,128)(2,1)S(1)} reshape(bf16[8,80,1408]{2,1,0:T(8,128)(2,1)} %get-tuple-element.30) | data formatting | bytes 3604480 | tf_op jit(solution)/shard_map/reshape | solution.py:95
  80.6 4.4 %all-to-all-start.2 = ((bf16[8,4,80,352]{3,2,0,1:T(8,128)(2,1)}), bf16[8,4,80,352]{3,2,0,1:T(8,128)(2,1)}, u32[]{:S(2)}, u32[]{:S(2)}) async-start(bf16[8,4,80,352]{3,2,0,1:T(8,128)(2,1)} %copy.76), calls=%async_computation.2 | async-start | bytes 3932160 | tf_op jit(solution)/shard_map/all_to_all | solution.py:96
  87.8 7.1 %update.4 = (f32[12160,128]{1,0:T(8,128)}, f32[12160,128]{1,0:T(8,128)}, f32[12160,128]{1,0:T(8,128)}, bf16[3840,128]{1,0:T(8,128)(2,1)}) custom-call(f32[1,1]{1,0:T(1,128)} %min.3.scale_ref, bf16[3840,128]{1,0:T(8,128)(2,1)} %reshape.97.gradient_ref, f32[12160,128]{1,0:T(8,128)} %bitcast.72, ...), custom_call_target="tpu_custom_call", output_to_operand_aliasing={{0}: (5, {}), {1}: (6, {}), {2}: (7, {})} | custom-call | tf_op jit(solution)/shard_map/update/pallas_call | solution.py:129
  94.9 5.9 %reshape.107 = bf16[8,4,384,40]{3,2,1,0:T(8,128)(2,1)S(1)} reshape(bf16[3840,128]{1,0:T(8,128)(2,1)} %get-tuple-element.41) | data formatting | bytes 1966080 | tf_op jit(solution)/shard_map/reshape | solution.py:182
  100.9 29.1 %all-to-all-done.2 = bf16[8,4,80,352]{3,2,0,1:T(8,128)(2,1)} async-done(((bf16[8,4,80,352]{3,2,0,1:T(8,128)(2,1)}), bf16[8,4,80,352]{3,2,0,1:T(8,128)(2,1)}, u32[]{:S(2)}, u32[]{:S(2)}) %all-to-all-start.2) | async-done | bytes 1802272 | tf_op jit(solution)/shard_map/all_to_all | solution.py:96
  130.0 3.0 %copy.77 = bf16[8,4,80,352]{3,2,1,0:T(8,128)(2,1)} copy(bf16[8,4,80,352]{3,2,0,1:T(8,128)(2,1)} %all-to-all-done.2) | data formatting | bytes 3604480 | tf_op jit(solution)/shard_map/all_to_all | solution.py:96
  133.1 5.7 %reshape.99.gradient_ref = bf16[7040,128]{1,0:T(8,128)(2,1)} reshape(bf16[8,4,80,352]{3,2,1,0:T(8,128)(2,1)} %copy.77) | data formatting | bytes 3604480 | tf_op jit(solution)/shard_map/reshape | solution.py:97
  141.0 3.7 %all-to-all-start.3 = ((bf16[8,4,384,40]{2,3,0,1:T(8,128)(2,1)}), bf16[8,4,384,40]{2,3,0,1:T(8,128)(2,1)S(1)}, u32[]{:S(2)}, u32[]{:S(2)}) async-start(bf16[8,4,384,40]{2,3,0,1:T(8,128)(2,1)} %copy.78), calls=%async_computation.3 | async-start | bytes 1966080 | tf_op jit(solution)/shard_map/all_to_all | solution.py:102
  144.7 13.3 %update.5 = (f32[12160,128]{1,0:T(8,128)}, f32[12160,128]{1,0:T(8,128)}, f32[12160,128]{1,0:T(8,128)}, bf16[7040,128]{1,0:T(8,128)(2,1)}) custom-call(f32[1,1]{1,0:T(1,128)} %min.3.scale_ref, bf16[7040,128]{1,0:T(8,128)(2,1)} %reshape.99.gradient_ref, f32[12160,128]{1,0:T(8,128)} %bitcast.73, ...), custom_call_target="tpu_custom_call", output_to_operand_aliasing={{0}: (5, {}), {1}: (6, {}), {2}: (7, {})} | custom-call | tf_op jit(solution)/shard_map/update/pallas_call | solution.py:129
  158.0 3.9 %reshape.106 = bf16[8,4,80,352]{3,2,1,0:T(8,128)(2,1)S(1)} reshape(bf16[7040,128]{1,0:T(8,128)(2,1)} %get-tuple-element.40) | data formatting | bytes 3604480 | tf_op jit(solution)/shard_map/reshape | solution.py:182
  161.9 6.4 %all-to-all-done.3 = bf16[8,4,384,40]{2,3,0,1:T(8,128)(2,1)S(1)} async-done(((bf16[8,4,384,40]{2,3,0,1:T(8,128)(2,1)}), bf16[8,4,384,40]{2,3,0,1:T(8,128)(2,1)S(1)}, u32[]{:S(2)}, u32[]{:S(2)}) %all-to-all-start.3) | async-done | bytes 983072 | tf_op jit(solution)/shard_map/all_to_all | solution.py:102
  170.9 3.7 %all-to-all-start.4 = ((bf16[8,4,80,352]{3,2,0,1:T(8,128)(2,1)}), bf16[8,4,80,352]{3,2,0,1:T(8,128)(2,1)S(1)}, u32[]{:S(2)}, u32[]{:S(2)}) async-start(bf16[8,4,80,352]{3,2,0,1:T(8,128)(2,1)} %copy.80), calls=%async_computation.4 | async-start | bytes 3932160 | tf_op jit(solution)/shard_map/all_to_all | solution.py:102
  177.6 41.9 %all-to-all-done.4 = bf16[8,4,80,352]{3,2,0,1:T(8,128)(2,1)S(1)} async-done(((bf16[8,4,80,352]{3,2,0,1:T(8,128)(2,1)}), bf16[8,4,80,352]{3,2,0,1:T(8,128)(2,1)S(1)}, u32[]{:S(2)}, u32[]{:S(2)}) %all-to-all-start.4) | async-done | bytes 1802272 | tf_op jit(solution)/shard_map/all_to_all | solution.py:102
  220.8 3.1 %copy.81 = bf16[8,1,80,4,352]{4,3,2,0,1:T(4,128)(2,1)S(1)} copy(bf16[8,1,80,4,352]{4,2,0,3,1:T(8,128)(2,1)} %bitcast.85) | data formatting | bytes 3604480 | tf_op jit(solution)/shard_map/all_to_all | solution.py:102
  227.3 3.5 %all-to-all-start.5 = ((bf16[1,4,1024,40]{2,3,0,1:T(8,128)(2,1)}), bf16[1,4,1024,40]{2,3,0,1:T(8,128)(2,1)S(1)}, u32[]{:S(2)}, u32[]{:S(2)}) async-start(bf16[1,4,1024,40]{2,3,0,1:T(8,128)(2,1)} %copy.82), calls=%async_computation.5 | async-start | bytes 655360 | tf_op jit(solution)/shard_map/all_to_all | solution.py:102
  235.5 3.8 %all-to-all-done.5 = bf16[1,4,1024,40]{2,3,0,1:T(8,128)(2,1)S(1)} async-done(((bf16[1,4,1024,40]{2,3,0,1:T(8,128)(2,1)}), bf16[1,4,1024,40]{2,3,0,1:T(8,128)(2,1)S(1)}, u32[]{:S(2)}, u32[]{:S(2)}) %all-to-all-start.5) | async-done | bytes 327712 | tf_op jit(solution)/shard_map/all_to_all | solution.py:102
  241.9 5.9 %multiply_add_fusion.1 = (f32[8,768,160]{1,2,0:T(8,128)}, bf16[8,768,160]{1,2,0:T(8,128)(2,1)}) fusion(f32[8,768,160]{1,2,0:T(8,128)} %param.21, bf16[8,384,160]{1,2,0:T(8,128)(2,1)} %get-tuple-element.62, bf16[8,384,160]{1,2,0:T(8,128)(2,1)S(1)} %get-tuple-element.61), kind=kLoop, calls=%fused_computation.1 | loop fusion | flops 7864320 | bytes 11796480 | tf_op jit(solution)/shard_map/add | solution.py:189
  251.9 5.0 %multiply_add_fusion = (f32[8,160,1408]{2,1,0:T(8,128)}, bf16[8,160,1408]{2,1,0:T(8,128)(2,1)}) fusion(f32[8,160,1408]{2,1,0:T(8,128)S(1)} %bitcast.87, bf16[8,80,1408]{2,1,0:T(8,128)(2,1)S(1)} %get-tuple-element.60, bf16[8,80,1408]{2,1,0:T(8,128)(2,1)S(1)} %get-tuple-element.59), kind=kLoop, calls=%fused_computation | loop fusion | flops 14417920 | bytes 21626880 | tf_op jit(solution)/shard_map/add | solution.py:189
  (83 shorter events, 67.0 us)
Async XLA Ops:
  1.7 3.6 %collective-permute-start.2 = (bf16[1,1024,160]{1,2,0:T(8,128)(2,1)S(1)}, bf16[1,1024,160]{1,2,0:T(8,128)(2,1)S(1)}, u32[]{:S(2)}, u32[]{:S(2)}) collective-permute-start(bf16[1,1024,160]{1,2,0:T(8,128)(2,1)S(1)} %constant_dynamic-slice_fusion), channel_id=1, source_target_pairs={{0,16},{16,0},{1,17},{17,1},{2,18},{18,2},{3,19},{19,3},{4,20},{20... | collective-permute-start | bytes 983048 | tf_op jit(solution)/shard_map/ppermute | solution.py:50
  4.7 23.4 %collective-permute-start.1 = (bf16[8,384,160]{1,0,2:T(8,128)(2,1)}, bf16[8,384,160]{1,0,2:T(8,128)(2,1)S(1)}, u32[]{:S(2)}, u32[]{:S(2)}) collective-permute-start(bf16[8,384,160]{1,0,2:T(8,128)(2,1)} %bitcast.69), channel_id=1, source_target_pairs={{0,16},{16,0},{1,17},{17,1},{2,18},{18,2},{3,19},{19,3},{4,20},{20... | collective-permute-start | bytes 2949128 | tf_op jit(solution)/shard_map/ppermute | solution.py:50
  10.5 14.3 %all-to-all-start = ((bf16[4,2,20480]{2,1,0:T(2,128)(2,1)}), bf16[4,2,20480]{2,1,0:T(2,128)(2,1)S(1)}, u32[]{:S(2)}, u32[]{:S(2)}) async-start(bf16[4,2,20480]{2,1,0:T(2,128)(2,1)} %reshape.114), calls=%async_computation | async-start | bytes 655360 | tf_op jit(solution)/shard_map/all_to_all | solution.py:93
  18.9 19.0 %collective-permute-start = (bf16[8,80,1408]{2,1,0:T(8,128)(2,1)}, bf16[8,80,1408]{2,1,0:T(8,128)(2,1)}, u32[]{:S(2)}, u32[]{:S(2)}) collective-permute-start(bf16[8,80,1408]{2,1,0:T(8,128)(2,1)} %dynamic-slice_bitcast_fusion), channel_id=1, source_target_pairs={{0,16},{16,0},{1,17},{17,1},{2,18},{18,2},{3,19},{19,3},{4,20},{20... | collective-permute-start | bytes 5406728 | tf_op jit(solution)/shard_map/ppermute | solution.py:50
  30.1 34.9 %all-to-all-start.1 = ((bf16[8,384,160]{1,0,2:T(8,128)(2,1)}), bf16[8,384,160]{1,0,2:T(8,128)(2,1)S(1)}, u32[]{:S(2)}, u32[]{:S(2)}) async-start(bf16[8,384,160]{1,0,2:T(8,128)(2,1)} %get-tuple-element.29), calls=%async_computation.1 | async-start | bytes 1966080 | tf_op jit(solution)/shard_map/all_to_all | solution.py:93
  33.8 3.5 %collective-permute-start.10 = (bf16[8,3072]{1,0:T(8,128)(2,1)S(1)}, bf16[8,3072]{1,0:T(8,128)(2,1)S(1)}, u32[]{:S(2)}, u32[]{:S(2)}) collective-permute-start(bf16[8,3072]{1,0:T(8,128)(2,1)S(1)} %bitcast.96), channel_id=1, source_target_pairs={{0,16},{16,0},{1,17},{17,1},{2,18},{18,2},{3,19},{19,3},{4,20},{20... | collective-permute-start | bytes 147464 | tf_op jit(solution)/shard_map/ppermute | solution.py:50
  44.6 1.4 collective-permute-start.3
  46.6 7.1 %collective-permute-start.5 = (f32[1,1]{1,0:T(1,128)}, f32[1,1]{1,0:T(1,128)}, u32[]{:S(2)}, u32[]{:S(2)}) collective-permute-start(f32[1,1]{1,0:T(1,128)} %add.99), channel_id=1, source_target_pairs={{0,2},{1,3},{2,0},{3,1},{4,6},{5,7},{6,4},{7,5},{8,10},{9,11},{10,... | collective-permute-start | bytes 20 | tf_op jit(solution)/shard_map/ppermute | solution.py:50
  48.6 5.0 %collective-permute-start.6 = (f32[1,1]{1,0:T(1,128)}, f32[1,1]{1,0:T(1,128)}, u32[]{:S(2)}, u32[]{:S(2)}) collective-permute-start(f32[1,1]{1,0:T(1,128)} %add.99), channel_id=1, source_target_pairs={{0,3},{1,2},{2,1},{3,0},{4,7},{5,6},{6,5},{7,4},{8,11},{9,10},{10,... | collective-permute-start | bytes 20 | tf_op jit(solution)/shard_map/ppermute | solution.py:50
  50.5 2.5 collective-permute-start.4
  54.9 8.2 %collective-permute-start.8 = (f32[1,1]{1,0:T(1,128)}, f32[1,1]{1,0:T(1,128)}, u32[]{:S(2)}, u32[]{:S(2)}) collective-permute-start(f32[1,1]{1,0:T(1,128)} %add.102), channel_id=1, source_target_pairs={{0,8},{4,12},{8,0},{12,4},{1,9},{5,13},{9,1},{13,5},{2,10},{6,14},... | collective-permute-start | bytes 20 | tf_op jit(solution)/shard_map/ppermute | solution.py:50
  58.2 4.9 %collective-permute-start.9 = (f32[1,1]{1,0:T(1,128)}, f32[1,1]{1,0:T(1,128)}, u32[]{:S(2)}, u32[]{:S(2)}) collective-permute-start(f32[1,1]{1,0:T(1,128)} %add.102), channel_id=1, source_target_pairs={{0,12},{4,8},{8,4},{12,0},{1,13},{5,9},{9,5},{13,1},{2,14},{6,10},... | collective-permute-start | bytes 20 | tf_op jit(solution)/shard_map/ppermute | solution.py:50
  59.9 2.5 collective-permute-start.7
  80.6 49.4 %all-to-all-start.2 = ((bf16[8,4,80,352]{3,2,0,1:T(8,128)(2,1)}), bf16[8,4,80,352]{3,2,0,1:T(8,128)(2,1)}, u32[]{:S(2)}, u32[]{:S(2)}) async-start(bf16[8,4,80,352]{3,2,0,1:T(8,128)(2,1)} %copy.76), calls=%async_computation.2 | async-start | bytes 3932160 | tf_op jit(solution)/shard_map/all_to_all | solution.py:96
  141.0 27.4 %all-to-all-start.3 = ((bf16[8,4,384,40]{2,3,0,1:T(8,128)(2,1)}), bf16[8,4,384,40]{2,3,0,1:T(8,128)(2,1)S(1)}, u32[]{:S(2)}, u32[]{:S(2)}) async-start(bf16[8,4,384,40]{2,3,0,1:T(8,128)(2,1)} %copy.78), calls=%async_computation.3 | async-start | bytes 1966080 | tf_op jit(solution)/shard_map/all_to_all | solution.py:102
  170.9 48.6 %all-to-all-start.4 = ((bf16[8,4,80,352]{3,2,0,1:T(8,128)(2,1)}), bf16[8,4,80,352]{3,2,0,1:T(8,128)(2,1)S(1)}, u32[]{:S(2)}, u32[]{:S(2)}) async-start(bf16[8,4,80,352]{3,2,0,1:T(8,128)(2,1)} %copy.80), calls=%async_computation.4 | async-start | bytes 3932160 | tf_op jit(solution)/shard_map/all_to_all | solution.py:102
  174.6 58.3 %collective-permute-start.12 = (bf16[8,384,160]{1,2,0:T(8,128)(2,1)}, bf16[8,384,160]{1,2,0:T(8,128)(2,1)}, u32[]{:S(2)}, u32[]{:S(2)}) collective-permute-start(bf16[8,384,160]{1,2,0:T(8,128)(2,1)} %bitcast.19), channel_id=1, source_target_pairs={{0,16},{16,0},{1,17},{17,1},{2,18},{18,2},{3,19},{19,3},{4,20},{20... | collective-permute-start | bytes 2949128 | tf_op jit(solution)/shard_map/ppermute | solution.py:50
  223.8 6.9 %copy-start.7 = (f32[8,3072]{1,0:T(8,128)S(1)}, f32[8,3072]{1,0:T(8,128)}, u32[]{:S(2)}) copy-start(f32[8,3072]{1,0:T(8,128)} %param.23) | copy-start | bytes 294916
  223.9 6.9 %copy-start.8 = (f32[8,3072]{1,0:T(8,128)S(1)}, f32[8,3072]{1,0:T(8,128)}, u32[]{:S(2)}) copy-start(f32[8,3072]{1,0:T(8,128)} %param.24) | copy-start | bytes 294916
  227.3 12.1 %all-to-all-start.5 = ((bf16[1,4,1024,40]{2,3,0,1:T(8,128)(2,1)}), bf16[1,4,1024,40]{2,3,0,1:T(8,128)(2,1)S(1)}, u32[]{:S(2)}, u32[]{:S(2)}) async-start(bf16[1,4,1024,40]{2,3,0,1:T(8,128)(2,1)} %copy.82), calls=%async_computation.5 | async-start | bytes 655360 | tf_op jit(solution)/shard_map/all_to_all | solution.py:102
  231.5 18.6 %collective-permute-start.11 = (bf16[8,80,1408]{2,1,0:T(8,128)(2,1)S(1)}, bf16[8,80,1408]{2,1,0:T(8,128)(2,1)}, u32[]{:S(2)}, u32[]{:S(2)}) collective-permute-start(bf16[8,80,1408]{2,1,0:T(8,128)(2,1)S(1)} %copy-done.1), channel_id=1, source_target_pairs={{0,16},{16,0},{1,17},{17,1},{2,18},{18,2},{3,19},{19,3},{4,20},{20... | collective-permute-start | bytes 5406728 | tf_op jit(solution)/shard_map/ppermute | solution.py:50
  239.4 8.5 %collective-permute-start.13 = (bf16[1,1024,160]{1,2,0:T(8,128)(2,1)S(1)}, bf16[1,1024,160]{1,2,0:T(8,128)(2,1)S(1)}, u32[]{:S(2)}, u32[]{:S(2)}) collective-permute-start(bf16[1,1024,160]{1,2,0:T(8,128)(2,1)S(1)} %bitcast.93), channel_id=1, source_target_pairs={{0,16},{16,0},{1,17},{17,1},{2,18},{18,2},{3,19},{19,3},{4,20},{20... | collective-permute-start | bytes 983048 | tf_op jit(solution)/shard_map/ppermute | solution.py:50
  241.9 6.9 %copy-start.3 = (f32[2048,160]{0,1:T(8,128)S(1)}, f32[2048,160]{0,1:T(8,128)}, u32[]{:S(2)}) copy-start(f32[2048,160]{0,1:T(8,128)} %param.22) | copy-start | bytes 3932164
  241.9 10.0 %slice-start = ((s8[7208960]{0:T(1024)(128)(4,1)}), s8[4194304]{0:T(1024)(128)(4,1)S(1)}, s32[]{:S(2)}) async-start(s8[7208960]{0:T(1024)(128)(4,1)} %bitcast.86), calls=%async_computation.6 | async-start | bytes 8388608
  (8 other events, 31.2 us)

commit v3 on v2

--- a/solution.py
+++ b/solution.py
@@ -87,20 +87,38 @@
     )
 
 
-def to_owner(part, row_count):
+def move(pieces):
+    return lax.all_to_all(pieces, "row", split_axis=0, concat_axis=0, tiled=True)
+
+
+def owner_pieces(part, row_count, narrow):
     layer_count, half, block_cols = part.shape
-    if half % LANES == 0:
-        arrived = lax.all_to_all(part, "row", split_axis=2, concat_axis=1, tiled=True)
+    split = part.reshape(layer_count, half, row_count, -1)
+    if narrow:
+        return split.transpose(2, 0, 3, 1)
+    return split.transpose(2, 0, 1, 3)
+
+
+def owner_rows(arrived, narrow):
+    if narrow:
+        arrived = arrived.transpose(1, 0, 3, 2)
     else:
-        pieces = part.reshape(layer_count, half, row_count, -1).transpose(0, 2, 1, 3)
-        arrived = lax.all_to_all(pieces, "row", split_axis=1, concat_axis=1, tiled=True)
+        arrived = arrived.transpose(1, 0, 2, 3)
     return arrived.reshape(-1, LANES)
 
 
-def to_holder(section, row_count):
-    layer_count, row_count, half, width = section.shape
-    block = lax.all_to_all(section, "row", split_axis=1, concat_axis=3, tiled=True)
-    return block.reshape(layer_count, half, width * row_count)
+def holder_pieces(section, narrow):
+    if narrow:
+        return section.transpose(1, 0, 3, 2)
+    return section.transpose(1, 0, 2, 3)
+
+
+def holder_block(arrived, narrow):
+    if narrow:
+        block = arrived.transpose(1, 3, 0, 2)
+    else:
+        block = arrived.transpose(1, 2, 0, 3)
+    return block.reshape(*block.shape[:2], -1)
 
 
 def update_body(scale_ref, gradient_ref, momentum_ref, variance_ref, master_ref, *refs):
@@ -162,33 +180,46 @@
     sums = [half_sum(matrix_block) for matrix_block in matrices]
     local_squares = sum(jnp.sum(jnp.square(part.astype(jnp.float32))) for part in sums)
     local_squares = local_squares.reshape(1, 1)
-    for axis in ("rep", "tp", "row"):
-        local_squares = all_sum(local_squares, axis)
-    clip_scale = clip_factor(local_squares + jnp.sum(gain_total * gain_total))
+    row_squares = all_sum(all_sum(local_squares, "rep"), "row")
+    clip_scale = clip_factor(all_sum(row_squares, "tp") + jnp.sum(gain_total * gain_total))
 
     flat = [array.reshape(-1, LANES) for array in (momentum, variance, master)]
     starts = [0, sums[0].size // LANES, (sums[0].size + sums[1].size) // LANES]
-    arrived = [None] * 3
-    arrived[2] = to_owner(sums[2], row_count)
-    arrived[1] = to_owner(after(sums[1], arrived[2]), row_count)
-    arrived[0] = to_owner(after(sums[0], arrived[1], clip_scale), row_count)
+    narrow = [part.shape[2] < part.shape[1] for part in sums]
+    pieces = [
+        owner_pieces(part, row_count, thin) for part, thin in zip(sums, narrow)
+    ]
+    moved = [None] * 3
+    moved[2] = move(pieces[2])
+    moved[1] = move(after(pieces[1], moved[2]))
+    moved[0] = move(after(pieces[0], moved[1], row_squares))
     carried = None
-    updated = [None] * 3
+    pieces = [None] * 3
     for k in (2, 1, 0):
         layer_count, half, block_cols = sums[k].shape
+        arrived = moved[k] if k == 0 else after(moved[k], clip_scale)
         *carried, weight = update_section(
-            clip_scale, arrived[k], *flat, starts[k], carried
+            clip_scale, owner_rows(arrived, narrow[k]), *flat, starts[k], carried
         )
-        updated[k] = weight.reshape(layer_count, row_count, half, block_cols // row_count)
-    blocks = [None] * 3
-    blocks[1] = to_holder(after(updated[1], arrived[0]), row_count)
-    blocks[0] = to_holder(after(updated[0], blocks[1]), row_count)
-    blocks[2] = to_holder(after(updated[2], blocks[0]), row_count)
-    weights = [both_halves(block) for block in blocks]
-    averaged = [
-        average_decay * average + (1.0 - average_decay) * weight.astype(jnp.float32)
-        for average, weight in zip(averages, weights)
-    ]
+        pieces[k] = holder_pieces(
+            weight.reshape(layer_count, row_count, half, block_cols // row_count), narrow[k]
+        )
+    back = [None] * 3
+    weights = [None] * 3
+    averaged = [None] * 3
+
+    def settle(k):
+        weights[k] = both_halves(holder_block(back[k], narrow[k]))
+        averaged[k] = average_decay * averages[k] + (1.0 - average_decay) * weights[k].astype(
+            jnp.float32
+        )
+
+    back[1] = move(after(pieces[1], moved[0]))
+    settle(1)
+    back[0] = move(after(pieces[0], back[1]))
+    back[2] = move(after(pieces[2], back[0], averaged[1]))
+    settle(0)
+    settle(2)
     fresh_gain, fresh_momentum, fresh_variance = adam_update(
         gain_total, gain_momentum, gain_variance, gain_master, clip_scale
     )

time: 258 us -> 216 us (0.84)
  waiting for transfers between devices: 90.6 us -> 55.4 us
  local copies, waits for them, and re-layouts: 60.2 us -> 53.3 us
    all_to_all x6, waiting for transfers between devices: 86.4 us -> 47.9 us  [move(): lax.all_to_all(pieces, 'row', split_axis=0, concat_axis=0, tiled=True)]
    all_to_all x5 -> x1, local copies, waits for them, and re-layouts: 10.6 us -> 1.04 us  [move(): lax.all_to_all(pieces, 'row', split_axis=0, concat_axis=0, tiled=True)]
    transpose x1 -> x4, local copies, waits for them, and re-layouts: 1.52 us -> 8.24 us  [the longest x2 3.4 us: owner_rows(): arrived = arrived.transpose(1, 0, 3, 2)]
    unnamed x28 -> x18, local copies, waits for them, and re-layouts: 4.13 us -> 0.72 us
    ppermute x14, waiting for transfers between devices: 4.25 us -> 7.51 us  [swap(): return lax.ppermute(moving, axis, [(i, i ^ distance) for i in range(count)])]
    reshape x3 -> x4, local copies, waits for them, and re-layouts: 11.4 us -> 12.9 us  [shards(): weight.reshape(layer_count, row_count, half, block_cols // row_count)]
    optimization_barrier x3 -> x4, local copies, waits for them, and re-layouts: 4.76 us -> 6.21 us  [after(): return lax.optimization_barrier((value, *earlier))[0]]
  transfers between devices with their start and end apart: 20 -> 20, of which waited for: 8 -> 8; matrix products, arithmetic and copies ran while one was open for 20% -> 31% of each run, Pallas kernels for 9% -> 11%
where the time goes in v3:
time: 216 us; the launch traced here: 214 us
  waiting for transfers between devices  55.4 us (26%)
  local copies, waits for them, and re-layouts  53.3 us (25%)
  starting transfers between devices  47.6 us (22%)
  other arithmetic  26.7 us (12%)
  Pallas kernels  23.1 us (11%)
  between operations  7.85 us (4%)
    all_to_all x6, waiting for transfers between devices, move(): lax.all_to_all(pieces, 'row', split_axis=0, concat_axis=0, tiled=True)  47.9 us
    all_to_all x6, starting transfers between devices, move(): lax.all_to_all(pieces, 'row', split_axis=0, concat_axis=0, tiled=True)  25.8 us
    pallas_call x3, Pallas kernels, update_section(): pl.pallas_call(update_body, grid=(rows // tile,), in_specs=[pl.BlockSpec(...  23.1 us
    ppermute x14, starting transfers between devices, swap(): return lax.ppermute(moving, axis, [(i, i ^ distance) for i in range(count)])  21.9 us
    reshape x4, local copies, waits for them, and re-layouts, shards(): weight.reshape(layer_count, row_count, half, block_cols // row_count)  12.9 us
    reshape x3, local copies, waits for them, and re-layouts, owner_rows(): return arrived.reshape(-1, LANES)  12.5 us
    add x3, other arithmetic, settle(): average_decay * averages[k]  11.7 us
    reduce_sum x3, other arithmetic, shards(): jnp.sum(jnp.square(part.astype(jnp.float32)))  9.46 us
  transfers between devices with their start and end apart: 20, of which 8 were waited for; matrix products, arithmetic and copies ran while one was open for 31% of the time, Pallas kernels for 11%

profile of v3, /device:TPU:1, one launch (start us, length us, event | category | flops | bytes accessed | tf_op | source)
XLA Modules:
  0.0 214.0 jit_solution(3294112909213811742)
XLA Ops:
  3.4 3.0 %dynamic-slice_bitcast_fusion = bf16[8,80,1408]{2,1,0:T(8,128)(2,1)} fusion(bf16[1,8,160,1408]{3,2,1,0:T(8,128)(2,1)} %param.13, s32[]{:T(128)S(6)} %select_n.55), kind=kLoop, calls=%fused_computation.11 | loop fusion | bytes 3604484 | tf_op jit(solution)/shard_map/dynamic_slice | solution.py:77
  8.8 6.1 %all-to-all-start = ((bf16[4,1,40,1024]{3,2,1,0:T(8,128)(2,1)}), bf16[4,1,40,1024]{3,2,1,0:T(8,128)(2,1)S(1)}, u32[]{:S(2)}, u32[]{:S(2)}) async-start(bf16[4,1,40,1024]{3,2,1,0:T(8,128)(2,1)} %bitcast.11), calls=%async_computation | async-start | bytes 655360 | tf_op jit(solution)/shard_map/all_to_all | solution.py:91
  17.2 7.7 %all-to-all-done = bf16[4,1,40,1024]{3,2,1,0:T(8,128)(2,1)S(1)} async-done(((bf16[4,1,40,1024]{3,2,1,0:T(8,128)(2,1)}), bf16[4,1,40,1024]{3,2,1,0:T(8,128)(2,1)S(1)}, u32[]{:S(2)}, u32[]{:S(2)}) %all-to-all-start) | async-done | bytes 327712 | tf_op jit(solution)/shard_map/all_to_all | solution.py:91
  26.0 3.5 %all-to-all-start.1 = ((bf16[4,8,40,384]{3,2,1,0:T(8,128)(2,1)}), bf16[4,8,40,384]{3,2,1,0:T(8,128)(2,1)S(1)}, u32[]{:S(2)}, u32[]{:S(2)}) async-start(bf16[4,8,40,384]{3,2,1,0:T(8,128)(2,1)} %copy.55), calls=%async_computation.1 | async-start | bytes 1966080 | tf_op jit(solution)/shard_map/all_to_all | solution.py:91
  29.5 4.7 %multiply_reduce_fusion = (f32[]{:T(128)}, bf16[8,80,1408]{2,1,0:T(8,128)(2,1)}) fusion(bf16[8,80,1408]{2,1,0:T(8,128)(2,1)} %collective-permute-done, bf16[1,8,160,1408]{3,2,1,0:T(8,128)(2,1)} %param.13, s32[]{:T(128)S(6)} %select_n.54), kind=kLoop, calls=%fused_computation.5 | loop fusion | flops 6307839 | bytes 5406728 | tf_op jit(solution)/shard_map/reduce_sum | solution.py:181
  38.3 4.3 %reshape.97 = bf16[8,80,4,352]{3,2,1,0:T(4,128)(2,1)S(1)} reshape(bf16[8,80,1408]{2,1,0:T(8,128)(2,1)} %get-tuple-element.62) | data formatting | bytes 3604480 | tf_op jit(solution)/shard_map/reshape | solution.py:96
  45.7 2.8 %collective-permute-start.5 = (f32[1,1]{1,0:T(1,128)}, f32[1,1]{1,0:T(1,128)}, u32[]{:S(2)}, u32[]{:S(2)}) collective-permute-start(f32[1,1]{1,0:T(1,128)} %add.99), channel_id=1, source_target_pairs={{0,8},{4,12},{8,0},{12,4},{1,9},{5,13},{9,1},{13,5},{2,10},{6,14},... | collective-permute-start | bytes 20 | tf_op jit(solution)/shard_map/ppermute | solution.py:50
  49.9 3.5 %collective-permute-done.5 = f32[1,1]{1,0:T(1,128)} collective-permute-done((f32[1,1]{1,0:T(1,128)}, f32[1,1]{1,0:T(1,128)}, u32[]{:S(2)}, u32[]{:S(2)}) %collective-permute-start.5) | collective-permute-done | bytes 36 | tf_op jit(solution)/shard_map/ppermute | solution.py:50
  56.3 4.5 %all-to-all-start.2 = ((bf16[4,8,80,352]{3,2,1,0:T(8,128)(2,1)}), bf16[4,8,80,352]{3,2,1,0:T(8,128)(2,1)}, u32[]{:S(2)}, u32[]{:S(2)}) async-start(bf16[4,8,80,352]{3,2,1,0:T(8,128)(2,1)} %copy.56), calls=%async_computation.2 | async-start | bytes 3932160 | tf_op jit(solution)/shard_map/all_to_all | solution.py:91
  79.8 2.9 %copy.58 = bf16[8,4,384,40]{3,2,1,0:T(8,128)(2,1)S(1)} copy(bf16[8,4,384,40]{2,3,0,1:T(8,128)(2,1)} %bitcast.84) | data formatting | bytes 1966080 | tf_op jit(solution)/shard_map/transpose | solution.py:104
  82.8 5.8 %reshape.104.gradient_ref = bf16[3840,128]{1,0:T(8,128)(2,1)} reshape(bf16[8,4,384,40]{3,2,1,0:T(8,128)(2,1)S(1)} %copy.58) | data formatting | bytes 1966080 | tf_op jit(solution)/shard_map/reshape | solution.py:107
  88.5 7.1 %update.4 = (f32[12160,128]{1,0:T(8,128)}, f32[12160,128]{1,0:T(8,128)}, f32[12160,128]{1,0:T(8,128)}, bf16[3840,128]{1,0:T(8,128)(2,1)}) custom-call(f32[1,1]{1,0:T(1,128)} %min.3.scale_ref, bf16[3840,128]{1,0:T(8,128)(2,1)} %reshape.104.gradient_ref, f32[12160,128]{1,0:T(8,128)} %bitcast.68, ...), custom_call_target="tpu_custom_call", output_to_operand_aliasing={{0}: (5, {}), {1}: (6, {}), {2}: (7, {})} | custom-call | tf_op jit(solution)/shard_map/update/pallas_call | solution.py:147
  95.7 5.9 %reshape.110 = bf16[8,4,384,40]{3,2,1,0:T(8,128)(2,1)S(1)} reshape(bf16[3840,128]{1,0:T(8,128)(2,1)} %get-tuple-element.45) | data formatting | bytes 1966080 | tf_op jit(solution)/shard_map/reshape | solution.py:205
  101.6 4.3 %all-to-all-done.2 = bf16[4,8,80,352]{3,2,1,0:T(8,128)(2,1)} async-done(((bf16[4,8,80,352]{3,2,1,0:T(8,128)(2,1)}), bf16[4,8,80,352]{3,2,1,0:T(8,128)(2,1)}, u32[]{:S(2)}, u32[]{:S(2)}) %all-to-all-start.2) | async-done | bytes 1802272 | tf_op jit(solution)/shard_map/all_to_all | solution.py:91
  108.1 3.7 %all-to-all-start.3 = ((bf16[4,8,40,384]{3,2,1,0:T(8,128)(2,1)}), bf16[4,8,40,384]{3,2,1,0:T(8,128)(2,1)S(1)}, u32[]{:S(2)}, u32[]{:S(2)}) async-start(bf16[4,8,40,384]{3,2,1,0:T(8,128)(2,1)} %copy.61), calls=%async_computation.3 | async-start | bytes 1966080 | tf_op jit(solution)/shard_map/all_to_all | solution.py:91
  113.6 4.3 %reshape.100.gradient_ref = bf16[7040,128]{1,0:T(8,128)(2,1)} reshape(bf16[8,4,80,352]{3,2,1,0:T(8,128)(2,1)S(1)} %copy.57) | data formatting | bytes 3604480 | tf_op jit(solution)/shard_map/reshape | solution.py:107
  117.9 13.3 %update.5 = (f32[12160,128]{1,0:T(8,128)}, f32[12160,128]{1,0:T(8,128)}, f32[12160,128]{1,0:T(8,128)}, bf16[7040,128]{1,0:T(8,128)(2,1)}) custom-call(f32[1,1]{1,0:T(1,128)} %min.3.scale_ref, bf16[7040,128]{1,0:T(8,128)(2,1)} %reshape.100.gradient_ref, f32[12160,128]{1,0:T(8,128)} %bitcast.69, ...), custom_call_target="tpu_custom_call", output_to_operand_aliasing={{0}: (5, {}), {1}: (6, {}), {2}: (7, {})} | custom-call | tf_op jit(solution)/shard_map/update/pallas_call | solution.py:147
  131.2 3.9 %reshape.109 = bf16[8,4,80,352]{3,2,1,0:T(8,128)(2,1)S(1)} reshape(bf16[7040,128]{1,0:T(8,128)(2,1)} %get-tuple-element.44) | data formatting | bytes 3604480 | tf_op jit(solution)/shard_map/reshape | solution.py:205
  136.6 4.5 %all-to-all-start.4 = ((bf16[4,8,80,352]{3,2,1,0:T(8,128)(2,1)}), bf16[4,8,80,352]{3,2,1,0:T(8,128)(2,1)S(1)}, u32[]{:S(2)}, u32[]{:S(2)}) async-start(bf16[4,8,80,352]{3,2,1,0:T(8,128)(2,1)} %bitcast.82), calls=%async_computation.4 | async-start | bytes 3932160 | tf_op jit(solution)/shard_map/all_to_all | solution.py:91
  148.5 3.4 %multiply_add_fusion.1 = (f32[8,768,160]{1,2,0:T(8,128)}, bf16[8,768,160]{1,2,0:T(8,128)(2,1)}) fusion(f32[8,768,160]{1,2,0:T(8,128)S(1)} %copy-done.2, bf16[8,384,160]{1,2,0:T(8,128)(2,1)S(1)} %get-tuple-element.66, bf16[8,384,160]{1,2,0:T(8,128)(2,1)S(1)} %get-tuple-element.65), kind=kLoop, calls=%fused_computation.1 | loop fusion | flops 7864320 | bytes 11796480 | tf_op jit(solution)/shard_map/add | solution.py:213
  151.9 34.1 %all-to-all-done.4 = bf16[4,8,80,352]{3,2,1,0:T(8,128)(2,1)S(1)} async-done(((bf16[4,8,80,352]{3,2,1,0:T(8,128)(2,1)}), bf16[4,8,80,352]{3,2,1,0:T(8,128)(2,1)S(1)}, u32[]{:S(2)}, u32[]{:S(2)}) %all-to-all-start.4) | async-done | bytes 1802272 | tf_op jit(solution)/shard_map/all_to_all | solution.py:91
  187.4 3.5 %all-to-all-start.5 = ((bf16[4,1,40,1024]{3,2,1,0:T(8,128)(2,1)}), bf16[4,1,40,1024]{3,2,1,0:T(8,128)(2,1)S(1)}, u32[]{:S(2)}, u32[]{:S(2)}) async-start(bf16[4,1,40,1024]{3,2,1,0:T(8,128)(2,1)} %copy.64), calls=%async_computation.5 | async-start | bytes 655360 | tf_op jit(solution)/shard_map/all_to_all | solution.py:91
  190.9 3.1 %copy.62 = bf16[8,80,4,352]{3,2,1,0:T(4,128)(2,1)S(1)} copy(bf16[8,80,4,352]{3,1,0,2:T(8,128)(2,1)} %bitcast.81) | data formatting | bytes 3604480 | tf_op jit(solution)/shard_map/transpose | solution.py:120
  207.0 7.0 %multiply_add_fusion = (f32[8,160,1408]{2,1,0:T(8,128)}, bf16[8,160,1408]{2,1,0:T(8,128)(2,1)}) fusion(f32[8,160,1408]{2,1,0:T(8,128)} %param.20, bf16[8,80,1408]{2,1,0:T(8,128)(2,1)S(1)} %get-tuple-element.64, bf16[8,80,1408]{2,1,0:T(8,128)(2,1)S(1)} %get-tuple-element.63), kind=kLoop, calls=%fused_computation | loop fusion | flops 14417920 | bytes 21626880 | tf_op jit(solution)/shard_map/add | solution.py:213
  (70 shorter events, 59.3 us)
Async XLA Ops:
  2.0 12.8 %collective-permute-start.1 = (bf16[8,384,160]{1,2,0:T(8,128)(2,1)S(1)}, bf16[8,384,160]{1,2,0:T(8,128)(2,1)}, u32[]{:S(2)}, u32[]{:S(2)}) collective-permute-start(bf16[8,384,160]{1,2,0:T(8,128)(2,1)S(1)} %dynamic-slice_bitcast_fusion.1), channel_id=1, source_target_pairs={{0,16},{16,0},{1,17},{17,1},{2,18},{18,2},{3,19},{19,3},{4,20},{20... | collective-permute-start | bytes 2949128 | tf_op jit(solution)/shard_map/ppermute | solution.py:50
  2.9 3.5 %collective-permute-start.2 = (bf16[1,1024,160]{1,2,0:T(8,128)(2,1)}, bf16[1,1024,160]{1,2,0:T(8,128)(2,1)S(1)}, u32[]{:S(2)}, u32[]{:S(2)}) collective-permute-start(bf16[1,1024,160]{1,2,0:T(8,128)(2,1)} %constant_dynamic-slice_fusion), channel_id=1, source_target_pairs={{0,16},{16,0},{1,17},{17,1},{2,18},{18,2},{3,19},{19,3},{4,20},{20... | collective-permute-start | bytes 983048 | tf_op jit(solution)/shard_map/ppermute | solution.py:50
  3.4 11.5 %copy-start.4 = (bf16[1,8,768,160]{2,3,1,0:T(8,128)(2,1)S(1)}, bf16[1,8,768,160]{2,3,1,0:T(8,128)(2,1)}, u32[]{:S(2)}) copy-start(bf16[1,8,768,160]{2,3,1,0:T(8,128)(2,1)} %param.14) | copy-start | bytes 5898244
  6.3 23.1 %collective-permute-start = (bf16[8,80,1408]{2,1,0:T(8,128)(2,1)}, bf16[8,80,1408]{2,1,0:T(8,128)(2,1)}, u32[]{:S(2)}, u32[]{:S(2)}) collective-permute-start(bf16[8,80,1408]{2,1,0:T(8,128)(2,1)} %dynamic-slice_bitcast_fusion), channel_id=1, source_target_pairs={{0,16},{16,0},{1,17},{17,1},{2,18},{18,2},{3,19},{19,3},{4,20},{20... | collective-permute-start | bytes 5406728 | tf_op jit(solution)/shard_map/ppermute | solution.py:50
  8.8 16.1 %all-to-all-start = ((bf16[4,1,40,1024]{3,2,1,0:T(8,128)(2,1)}), bf16[4,1,40,1024]{3,2,1,0:T(8,128)(2,1)S(1)}, u32[]{:S(2)}, u32[]{:S(2)}) async-start(bf16[4,1,40,1024]{3,2,1,0:T(8,128)(2,1)} %bitcast.11), calls=%async_computation | async-start | bytes 655360 | tf_op jit(solution)/shard_map/all_to_all | solution.py:91
  26.0 28.8 %all-to-all-start.1 = ((bf16[4,8,40,384]{3,2,1,0:T(8,128)(2,1)}), bf16[4,8,40,384]{3,2,1,0:T(8,128)(2,1)S(1)}, u32[]{:S(2)}, u32[]{:S(2)}) async-start(bf16[4,8,40,384]{3,2,1,0:T(8,128)(2,1)} %copy.55), calls=%async_computation.1 | async-start | bytes 1966080 | tf_op jit(solution)/shard_map/all_to_all | solution.py:91
  36.2 6.5 %collective-permute-start.3 = (f32[1,1]{1,0:T(1,128)}, f32[1,1]{1,0:T(1,128)}, u32[]{:S(2)}, u32[]{:S(2)}) collective-permute-start(f32[1,1]{1,0:T(1,128)} %bitcast.4), channel_id=1, source_target_pairs={{0,16},{16,0},{1,17},{17,1},{2,18},{18,2},{3,19},{19,3},{4,20},{20... | collective-permute-start | bytes 20 | tf_op jit(solution)/shard_map/ppermute | solution.py:50
  43.3 6.0 %collective-permute-start.4 = (f32[1,1]{1,0:T(1,128)}, f32[1,1]{1,0:T(1,128)}, u32[]{:S(2)}, u32[]{:S(2)}) collective-permute-start(f32[1,1]{1,0:T(1,128)} %add.99), channel_id=1, source_target_pairs={{0,4},{4,0},{8,12},{12,8},{1,5},{5,1},{9,13},{13,9},{2,6},{6,2},{1... | collective-permute-start | bytes 20 | tf_op jit(solution)/shard_map/ppermute | solution.py:50
  45.7 7.6 %collective-permute-start.5 = (f32[1,1]{1,0:T(1,128)}, f32[1,1]{1,0:T(1,128)}, u32[]{:S(2)}, u32[]{:S(2)}) collective-permute-start(f32[1,1]{1,0:T(1,128)} %add.99), channel_id=1, source_target_pairs={{0,8},{4,12},{8,0},{12,4},{1,9},{5,13},{9,1},{13,5},{2,10},{6,14},... | collective-permute-start | bytes 20 | tf_op jit(solution)/shard_map/ppermute | solution.py:50
  48.6 4.8 %collective-permute-start.6 = (f32[1,1]{1,0:T(1,128)}, f32[1,1]{1,0:T(1,128)}, u32[]{:S(2)}, u32[]{:S(2)}) collective-permute-start(f32[1,1]{1,0:T(1,128)} %add.99), channel_id=1, source_target_pairs={{0,12},{4,8},{8,4},{12,0},{1,13},{5,9},{9,5},{13,1},{2,14},{6,10},... | collective-permute-start | bytes 20 | tf_op jit(solution)/shard_map/ppermute | solution.py:50
  56.3 4.6 %copy-start.8 = (bf16[1,8,3072]{2,1,0:T(8,128)(2,1)S(1)}, bf16[1,8,3072]{2,1,0:T(8,128)(2,1)}, u32[]{:S(2)}) copy-start(bf16[1,8,3072]{2,1,0:T(8,128)(2,1)} %param.16) | copy-start | bytes 147460
  56.3 49.6 %all-to-all-start.2 = ((bf16[4,8,80,352]{3,2,1,0:T(8,128)(2,1)}), bf16[4,8,80,352]{3,2,1,0:T(8,128)(2,1)}, u32[]{:S(2)}, u32[]{:S(2)}) async-start(bf16[4,8,80,352]{3,2,1,0:T(8,128)(2,1)} %copy.56), calls=%async_computation.2 | async-start | bytes 3932160 | tf_op jit(solution)/shard_map/all_to_all | solution.py:91
  60.9 3.2 %collective-permute-start.10 = (bf16[8,3072]{1,0:T(8,128)(2,1)S(1)}, bf16[8,3072]{1,0:T(8,128)(2,1)S(1)}, u32[]{:S(2)}, u32[]{:S(2)}) collective-permute-start(bf16[8,3072]{1,0:T(8,128)(2,1)S(1)} %bitcast.91), channel_id=1, source_target_pairs={{0,16},{16,0},{1,17},{17,1},{2,18},{18,2},{3,19},{19,3},{4,20},{20... | collective-permute-start | bytes 147464 | tf_op jit(solution)/shard_map/ppermute | solution.py:50
  64.7 4.8 %collective-permute-start.7 = (f32[1,1]{1,0:T(1,128)}, f32[1,1]{1,0:T(1,128)}, u32[]{:S(2)}, u32[]{:S(2)}) collective-permute-start(f32[1,1]{1,0:T(1,128)} %add.102), channel_id=1, source_target_pairs={{0,1},{1,0},{2,3},{3,2},{4,5},{5,4},{6,7},{7,6},{8,9},{9,8},{10,11... | collective-permute-start | bytes 20 | tf_op jit(solution)/shard_map/ppermute | solution.py:50
  66.6 3.5 %collective-permute-start.8 = (f32[1,1]{1,0:T(1,128)}, f32[1,1]{1,0:T(1,128)}, u32[]{:S(2)}, u32[]{:S(2)}) collective-permute-start(f32[1,1]{1,0:T(1,128)} %add.102), channel_id=1, source_target_pairs={{0,2},{1,3},{2,0},{3,1},{4,6},{5,7},{6,4},{7,5},{8,10},{9,11},{10,... | collective-permute-start | bytes 20 | tf_op jit(solution)/shard_map/ppermute | solution.py:50
  68.6 3.7 %collective-permute-start.9 = (f32[1,1]{1,0:T(1,128)}, f32[1,1]{1,0:T(1,128)}, u32[]{:S(2)}, u32[]{:S(2)}) collective-permute-start(f32[1,1]{1,0:T(1,128)} %add.102), channel_id=1, source_target_pairs={{0,3},{1,2},{2,1},{3,0},{4,7},{5,6},{6,5},{7,4},{8,11},{9,10},{10,... | collective-permute-start | bytes 20 | tf_op jit(solution)/shard_map/ppermute | solution.py:50
  108.1 28.5 %all-to-all-start.3 = ((bf16[4,8,40,384]{3,2,1,0:T(8,128)(2,1)}), bf16[4,8,40,384]{3,2,1,0:T(8,128)(2,1)S(1)}, u32[]{:S(2)}, u32[]{:S(2)}) async-start(bf16[4,8,40,384]{3,2,1,0:T(8,128)(2,1)} %copy.61), calls=%async_computation.3 | async-start | bytes 1966080 | tf_op jit(solution)/shard_map/all_to_all | solution.py:91
  136.6 49.4 %all-to-all-start.4 = ((bf16[4,8,80,352]{3,2,1,0:T(8,128)(2,1)}), bf16[4,8,80,352]{3,2,1,0:T(8,128)(2,1)S(1)}, u32[]{:S(2)}, u32[]{:S(2)}) async-start(bf16[4,8,80,352]{3,2,1,0:T(8,128)(2,1)} %bitcast.82), calls=%async_computation.4 | async-start | bytes 3932160 | tf_op jit(solution)/shard_map/all_to_all | solution.py:91
  142.1 4.5 %collective-permute-start.12 = (bf16[8,384,160]{1,2,0:T(8,128)(2,1)}, bf16[8,384,160]{1,2,0:T(8,128)(2,1)}, u32[]{:S(2)}, u32[]{:S(2)}) collective-permute-start(bf16[8,384,160]{1,2,0:T(8,128)(2,1)} %bitcast.25), channel_id=1, source_target_pairs={{0,16},{16,0},{1,17},{17,1},{2,18},{18,2},{3,19},{19,3},{4,20},{20... | collective-permute-start | bytes 2949128 | tf_op jit(solution)/shard_map/ppermute | solution.py:50
  186.0 4.8 %copy-start = (bf16[4,8,80,352]{3,2,1,0:T(8,128)(2,1)}, bf16[4,8,80,352]{3,2,1,0:T(8,128)(2,1)S(1)}, u32[]{:S(2)}) copy-start(bf16[4,8,80,352]{3,2,1,0:T(8,128)(2,1)S(1)} %all-to-all-done.4) | copy-start | bytes 5406724
  187.4 12.1 %all-to-all-start.5 = ((bf16[4,1,40,1024]{3,2,1,0:T(8,128)(2,1)}), bf16[4,1,40,1024]{3,2,1,0:T(8,128)(2,1)S(1)}, u32[]{:S(2)}, u32[]{:S(2)}) async-start(bf16[4,1,40,1024]{3,2,1,0:T(8,128)(2,1)} %copy.64), calls=%async_computation.5 | async-start | bytes 655360 | tf_op jit(solution)/shard_map/all_to_all | solution.py:91
  196.3 8.5 %copy-start.5 = (f32[2048,160]{0,1:T(8,128)S(1)}, f32[2048,160]{0,1:T(8,128)}, u32[]{:S(2)}) copy-start(f32[2048,160]{0,1:T(8,128)} %param.22) | copy-start | bytes 3932164
  196.3 9.7 %collective-permute-start.11 = (bf16[8,80,1408]{2,1,0:T(8,128)(2,1)}, bf16[8,80,1408]{2,1,0:T(8,128)(2,1)S(1)}, u32[]{:S(2)}, u32[]{:S(2)}) collective-permute-start(bf16[8,80,1408]{2,1,0:T(8,128)(2,1)} %reshape.111), channel_id=1, source_target_pairs={{0,16},{16,0},{1,17},{17,1},{2,18},{18,2},{3,19},{19,3},{4,20},{20... | collective-permute-start | bytes 5406728 | tf_op jit(solution)/shard_map/ppermute | solution.py:50
  199.5 4.3 %collective-permute-start.13 = (bf16[1,1024,160]{1,2,0:T(8,128)(2,1)S(1)}, bf16[1,1024,160]{1,2,0:T(8,128)(2,1)S(1)}, u32[]{:S(2)}, u32[]{:S(2)}) collective-permute-start(bf16[1,1024,160]{1,2,0:T(8,128)(2,1)S(1)} %bitcast.89), channel_id=1, source_target_pairs={{0,16},{16,0},{1,17},{17,1},{2,18},{18,2},{3,19},{19,3},{4,20},{20... | collective-permute-start | bytes 983048 | tf_op jit(solution)/shard_map/ppermute | solution.py:50
  (5 other events, 10.9 us)

commit v4 on v3

--- a/solution.py
+++ b/solution.py
@@ -70,13 +70,71 @@
     return lax.optimization_barrier((value, *earlier))[0]
 
 
-def half_sum(matrix_block):
+def halves(matrix_block):
     half = matrix_block.shape[1] // lax.axis_size("rep")
     mine = lax.axis_index("rep")
     kept = lax.dynamic_slice_in_dim(matrix_block, mine * half, half, 1)
     sent = lax.dynamic_slice_in_dim(matrix_block, (1 - mine) * half, half, 1)
-    arrived = swap(sent, "rep", 1)
-    return (kept.astype(jnp.float32) + arrived.astype(jnp.float32)).astype(jnp.bfloat16)
+    return kept, swap(sent, "rep", 1)
+
+
+def half_sum(kept, arrived):
+    total = (kept.astype(jnp.float32) + arrived.astype(jnp.float32)).astype(jnp.bfloat16)
+    return total, jnp.sum(jnp.square(total.astype(jnp.float32)))
+
+
+def thin_body(kept_ref, arrived_ref, *refs):
+    pieces_ref, squares_ref = refs[-2:]
+    row_count, chunks, width, lanes = pieces_ref.shape
+    total = kept_ref[0].astype(jnp.float32) + arrived_ref[0].astype(jnp.float32)
+    total = total.astype(jnp.bfloat16).astype(jnp.float32)
+    squares_ref[0] = jnp.sum(total * total, axis=0, keepdims=True)
+    for r in range(row_count):
+        for c in range(chunks):
+            piece = total[r * width : (r + 1) * width, c * lanes : (c + 1) * lanes]
+            pieces_ref[r, c] = piece.astype(jnp.bfloat16)
+
+
+def thin_sum(kept, arrived, row_count, lanes, count, start, carried):
+    layer_count, half, block_cols = kept.shape
+    chunks = half // lanes
+    first = start // chunks
+    whole = pl.BlockSpec((1, block_cols, half), lambda i: (i, 0, 0))
+    width = block_cols // row_count
+    extra = [] if carried is None else [carried]
+    pieces, squares = pl.pallas_call(
+        thin_body,
+        grid=(layer_count,),
+        in_specs=[whole, whole] + [pl.BlockSpec(memory_space=pl.ANY) for _ in extra],
+        out_specs=[
+            pl.BlockSpec((row_count, chunks, width, lanes), lambda i: (0, i + first, 0, 0)),
+            pl.BlockSpec((1, 1, half), lambda i: (i, 0, 0)),
+        ],
+        out_shape=[
+            jax.ShapeDtypeStruct((row_count, count, width, lanes), jnp.bfloat16),
+            jax.ShapeDtypeStruct((layer_count, 1, half), jnp.float32),
+        ],
+        input_output_aliases={2 + k: k for k in range(len(extra))},
+        name="thin_sum",
+    )(kept.transpose(0, 2, 1), arrived.transpose(0, 2, 1), *extra)
+    return pieces, jnp.sum(squares)
+
+
+def thin_join(exit_pair, embed_pair, row_count):
+    counts = []
+    lanes = math.gcd(exit_pair[0].shape[1], embed_pair[0].shape[1])
+    for kept, _ in (exit_pair, embed_pair):
+        counts.append(kept.shape[0] * kept.shape[1] // lanes)
+    embed_chunks = embed_pair[0].shape[1] // lanes
+    width = embed_pair[0].shape[2] // row_count
+    if lanes % LANES == 0 and width % 8 == 0 and counts[0] % embed_chunks == 0:
+        joined, one = thin_sum(*exit_pair, row_count, lanes, sum(counts), 0, None)
+        joined, two = thin_sum(*embed_pair, row_count, lanes, sum(counts), counts[0], joined)
+        return joined, one + two, counts[0]
+    exit_total, one = half_sum(*exit_pair)
+    embed_total, two = half_sum(*embed_pair)
+    thin = [thin_pieces(part, row_count, lanes) for part in (exit_total, embed_total)]
+    return jnp.concatenate(thin, axis=1), one + two, counts[0]
 
 
 def both_halves(half):
@@ -91,20 +149,21 @@
     return lax.all_to_all(pieces, "row", split_axis=0, concat_axis=0, tiled=True)
 
 
-def owner_pieces(part, row_count, narrow):
+def owner_pieces(part, row_count):
     layer_count, half, block_cols = part.shape
-    split = part.reshape(layer_count, half, row_count, -1)
-    if narrow:
-        return split.transpose(2, 0, 3, 1)
-    return split.transpose(2, 0, 1, 3)
-
-
-def owner_rows(arrived, narrow):
-    if narrow:
-        arrived = arrived.transpose(1, 0, 3, 2)
-    else:
-        arrived = arrived.transpose(1, 0, 2, 3)
-    return arrived.reshape(-1, LANES)
+    return part.reshape(layer_count, half, row_count, -1).transpose(2, 0, 1, 3)
+
+
+def thin_pieces(part, row_count, lanes):
+    layer_count, half, block_cols = part.shape
+    split = part.reshape(layer_count, half // lanes, lanes, row_count, -1)
+    return split.transpose(3, 0, 1, 4, 2).reshape(row_count, -1, split.shape[4], lanes)
+
+
+def thin_rows(arrived, part):
+    row_count, _, width, lanes = arrived.shape
+    split = arrived.reshape(row_count, part.shape[0], -1, width, lanes)
+    return split.transpose(1, 0, 2, 4, 3).reshape(-1, LANES)
 
 
 def holder_pieces(section, narrow):
@@ -177,30 +236,30 @@
     gain_local = gain_gradient[0]
     gain_total = gain_local.astype(jnp.float32) + swap(gain_local, "rep", 1).astype(jnp.float32)
     gain_total = gain_total.astype(jnp.bfloat16).astype(jnp.float32)
-    sums = [half_sum(matrix_block) for matrix_block in matrices]
-    local_squares = sum(jnp.sum(jnp.square(part.astype(jnp.float32))) for part in sums)
-    local_squares = local_squares.reshape(1, 1)
+    pairs = [halves(matrix_block) for matrix_block in matrices]
+    thin, local_squares, split = thin_join(pairs[1], pairs[2], row_count)
+    entry_total, entry_squares = half_sum(*pairs[0])
+    local_squares = (local_squares + entry_squares).reshape(1, 1)
     row_squares = all_sum(all_sum(local_squares, "rep"), "row")
     clip_scale = clip_factor(all_sum(row_squares, "tp") + jnp.sum(gain_total * gain_total))
 
     flat = [array.reshape(-1, LANES) for array in (momentum, variance, master)]
-    starts = [0, sums[0].size // LANES, (sums[0].size + sums[1].size) // LANES]
-    narrow = [part.shape[2] < part.shape[1] for part in sums]
-    pieces = [
-        owner_pieces(part, row_count, thin) for part, thin in zip(sums, narrow)
+    parts = [kept for kept, _ in pairs]
+    starts = [0, parts[0].size // LANES, (parts[0].size + parts[1].size) // LANES]
+    narrow = [part.shape[2] < part.shape[1] for part in parts]
+    thin_moved = move(thin)
+    entry_moved = move(after(owner_pieces(entry_total, row_count), thin_moved, row_squares))
+    thin_arrived = after(thin_moved, clip_scale)
+    rows = [
+        entry_moved.transpose(1, 0, 2, 3).reshape(-1, LANES),
+        thin_rows(thin_arrived[:, :split], parts[1]),
+        thin_rows(thin_arrived[:, split:], parts[2]),
     ]
-    moved = [None] * 3
-    moved[2] = move(pieces[2])
-    moved[1] = move(after(pieces[1], moved[2]))
-    moved[0] = move(after(pieces[0], moved[1], row_squares))
     carried = None
     pieces = [None] * 3
     for k in (2, 1, 0):
-        layer_count, half, block_cols = sums[k].shape
-        arrived = moved[k] if k == 0 else after(moved[k], clip_scale)
-        *carried, weight = update_section(
-            clip_scale, owner_rows(arrived, narrow[k]), *flat, starts[k], carried
-        )
+        layer_count, half, block_cols = parts[k].shape
+        *carried, weight = update_section(clip_scale, rows[k], *flat, starts[k], carried)
         pieces[k] = holder_pieces(
             weight.reshape(layer_count, row_count, half, block_cols // row_count), narrow[k]
         )
@@ -214,7 +273,7 @@
             jnp.float32
         )
 
-    back[1] = move(after(pieces[1], moved[0]))
+    back[1] = move(after(pieces[1], entry_moved))
     settle(1)
     back[0] = move(after(pieces[0], back[1]))
     back[2] = move(after(pieces[2], back[0], averaged[1]))

time: 216 us -> 217 us (level)
  Pallas kernels: 23.1 us -> 30.9 us
  waiting for transfers between devices: 55.4 us -> 47.7 us
  local copies, waits for them, and re-layouts: 53.3 us -> 57.7 us
  other arithmetic: 26.7 us -> 22.6 us
    all_to_all x6 -> x5, waiting for transfers between devices: 47.9 us -> 39 us  [move(): lax.all_to_all(pieces, 'row', split_axis=0, concat_axis=0, tiled=True)]
    pallas_call x0 -> x2, Pallas kernels: none -> 7.76 us  [thin_sum(): pl.pallas_call(thin_body, grid=(layer_count,), in_specs=[whole, whole] +...]
    ppermute x14, starting transfers between devices: 21.9 us -> 26.2 us  [swap(): return lax.ppermute(moving, axis, [(i, i ^ distance) for i in range(count)])]
    reduce_sum x3, other arithmetic: 9.46 us -> 5.41 us  [the longest x1 4.18 us: half_sum(): return (total, jnp.sum(jnp.square(total.astype(jnp.float32))))]
    all_to_all x6 -> x5, starting transfers between devices: 25.8 us -> 22.2 us  [move(): lax.all_to_all(pieces, 'row', split_axis=0, concat_axis=0, tiled=True)]
    reshape x4 -> x5, local copies, waits for them, and re-layouts: 16.8 us -> 19.8 us  [the longest x2 8.14 us: thin_rows(): return split.transpose(1, 0, 2, 4, 3).reshape(-1, LANES)]
    optimization_barrier x4 -> x3, local copies, waits for them, and re-layouts: 6.21 us -> 5.26 us  [after(): return lax.optimization_barrier((value, *earlier))[0]]
  transfers between devices with their start and end apart: 20 -> 19, of which waited for: 8 -> 7; matrix products, arithmetic and copies ran while one was open for 31% -> 29% of each run, Pallas kernels for 11% -> 14%
where the time goes in v4:
time: 217 us; the launch traced here: 215 us
  local copies, waits for them, and re-layouts  57.7 us (27%)
  starting transfers between devices  48.4 us (22%)
  waiting for transfers between devices  47.7 us (22%)
  Pallas kernels  30.9 us (14%)
  other arithmetic  22.6 us (10%)
  between operations  7.9 us (4%)
    all_to_all x5, waiting for transfers between devices, move(): lax.all_to_all(pieces, 'row', split_axis=0, concat_axis=0, tiled=True)  39 us
    ppermute x14, starting transfers between devices, swap(): return lax.ppermute(moving, axis, [(i, i ^ distance) for i in range(count)])  26.2 us
    pallas_call x3, Pallas kernels, update_section(): pl.pallas_call(update_body, grid=(rows // tile,), in_specs=[pl.BlockSpec(...  23.1 us
    all_to_all x5, starting transfers between devices, move(): lax.all_to_all(pieces, 'row', split_axis=0, concat_axis=0, tiled=True)  22.2 us
    reshape x4, local copies, waits for them, and re-layouts, shards(): weight.reshape(layer_count, row_count, half, block_cols // row_count)  12.9 us
    add x3, other arithmetic, settle(): average_decay * averages[k]  11.7 us
    ppermute x14, waiting for transfers between devices, swap(): return lax.ppermute(moving, axis, [(i, i ^ distance) for i in range(count)])  8.63 us
    reshape x2, local copies, waits for them, and re-layouts, thin_rows(): return split.transpose(1, 0, 2, 4, 3).reshape(-1, LANES)  8.14 us
  transfers between devices with their start and end apart: 19, of which 7 were waited for; matrix products, arithmetic and copies ran while one was open for 29% of the time, Pallas kernels for 14%

profile of v4, /device:TPU:1, one launch (start us, length us, event | category | flops | bytes accessed | tf_op | source)
XLA Modules:
  0.0 215.2 jit_solution(5555249485851454216)
XLA Ops:
  0.7 3.0 %dynamic-slice_bitcast_fusion.1 = (bf16[8,384,160]{1,2,0:T(8,128)(2,1)}, bf16[8,160,384]{2,1,0:T(8,128)(2,1)}) fusion(bf16[1,8,768,160]{2,3,1,0:T(8,128)(2,1)} %param.14, s32[]{:T(128)S(6)} %select_n.55, s32[]{:T(128)S(6)} %select_n.54), kind=kLoop, calls=%fused_computation.12 | loop fusion | bytes 3932168 | tf_op jit(solution)/shard_map/dynamic_slice | solution.py:77
  8.8 5.7 %thin_sum.2 = (bf16[4,32,40,128]{3,2,1,0:T(8,128)(2,1)}, f32[8,1,384]{2,1,0:T(1,128)}) custom-call(bf16[8,160,384]{2,1,0:T(8,128)(2,1)} %get-tuple-element.68.kept_ref, bf16[8,160,384]{2,1,0:T(8,128)(2,1)} %bitcast.92), custom_call_target="tpu_custom_call" | custom-call | tf_op jit(solution)/shard_map/thin_sum/pallas_call | solution.py:105
  17.3 6.2 %all-to-all-start = ((bf16[4,32,40,128]{3,2,1,0:T(8,128)(2,1)}), bf16[4,32,40,128]{3,2,1,0:T(8,128)(2,1)S(1)}, u32[]{:S(2)}, u32[]{:S(2)}) async-start(bf16[4,32,40,128]{3,2,1,0:T(8,128)(2,1)} %get-tuple-element.36), calls=%async_computation | async-start | bytes 2621440 | tf_op jit(solution)/shard_map/all_to_all | solution.py:149
  26.0 4.2 %multiply_reduce_fusion = (f32[]{:T(128)}, bf16[8,80,1408]{2,1,0:T(8,128)(2,1)}) fusion(bf16[8,80,1408]{2,1,0:T(8,128)(2,1)S(1)} %collective-permute-done.2, bf16[1,8,160,1408]{3,2,1,0:T(8,128)(2,1)} %param.13, s32[]{:T(128)S(6)} %select_n.58), kind=kLoop, calls=%fused_computation.5 | loop fusion | flops 6307839 | bytes 5406728 | tf_op jit(solution)/shard_map/reduce_sum | solution.py:83
  32.2 4.3 %reshape.95 = bf16[8,80,4,352]{3,2,1,0:T(4,128)(2,1)S(1)} reshape(bf16[8,80,1408]{2,1,0:T(8,128)(2,1)} %get-tuple-element.62) | data formatting | bytes 3604480 | tf_op jit(solution)/shard_map/reshape | solution.py:154
  37.1 7.9 %collective-permute-start.4 = (f32[1,1]{1,0:T(1,128)}, f32[1,1]{1,0:T(1,128)}, u32[]{:S(2)}, u32[]{:S(2)}) collective-permute-start(f32[1,1]{1,0:T(1,128)} %add.91), channel_id=1, source_target_pairs={{0,4},{4,0},{8,12},{12,8},{1,5},{5,1},{9,13},{13,9},{2,6},{6,2},{1... | collective-permute-start | bytes 20 | tf_op jit(solution)/shard_map/ppermute | solution.py:50
  45.7 3.7 %collective-permute-start.6 = (f32[1,1]{1,0:T(1,128)}, f32[1,1]{1,0:T(1,128)}, u32[]{:S(2)}, u32[]{:S(2)}) collective-permute-start(f32[1,1]{1,0:T(1,128)} %add.91), channel_id=1, source_target_pairs={{0,12},{4,8},{8,4},{12,0},{1,13},{5,9},{9,5},{13,1},{2,14},{6,10},... | collective-permute-start | bytes 20 | tf_op jit(solution)/shard_map/ppermute | solution.py:50
  50.0 4.7 %collective-permute-done.5 = f32[1,1]{1,0:T(1,128)} collective-permute-done((f32[1,1]{1,0:T(1,128)}, f32[1,1]{1,0:T(1,128)}, u32[]{:S(2)}, u32[]{:S(2)}) %collective-permute-start.5) | collective-permute-done | bytes 36 | tf_op jit(solution)/shard_map/ppermute | solution.py:50
  57.6 4.6 %all-to-all-start.1 = ((bf16[4,8,80,352]{3,2,1,0:T(8,128)(2,1)}), bf16[4,8,80,352]{3,2,1,0:T(8,128)(2,1)}, u32[]{:S(2)}, u32[]{:S(2)}) async-start(bf16[4,8,80,352]{3,2,1,0:T(8,128)(2,1)} %copy.56), calls=%async_computation.1 | async-start | bytes 3932160 | tf_op jit(solution)/shard_map/all_to_all | solution.py:149
  75.7 2.9 %copy.58 = bf16[4,8,3,40,128]{3,4,2,0,1:T(8,128)(2,1)S(1)} copy(bf16[4,8,3,40,128]{4,3,2,1,0:T(8,128)(2,1)} %bitcast.87) | data formatting | bytes 1966080 | tf_op jit(solution)/shard_map/reshape | solution.py:165
  78.6 5.8 %reshape.101.gradient_ref = bf16[3840,128]{1,0:T(8,128)(2,1)} reshape(bf16[8,4,3,128,40]{4,3,2,1,0:T(8,128)(2,1)S(1)} %bitcast.82) | data formatting | bytes 1966080 | tf_op jit(solution)/shard_map/reshape | solution.py:166
  91.0 7.1 %update.4 = (f32[12160,128]{1,0:T(8,128)}, f32[12160,128]{1,0:T(8,128)}, f32[12160,128]{1,0:T(8,128)}, bf16[3840,128]{1,0:T(8,128)(2,1)}) custom-call(f32[1,1]{1,0:T(1,128)} %min.3.scale_ref, bf16[3840,128]{1,0:T(8,128)(2,1)} %reshape.101.gradient_ref, f32[12160,128]{1,0:T(8,128)} %bitcast.70, ...), custom_call_target="tpu_custom_call", output_to_operand_aliasing={{0}: (5, {}), {1}: (6, {}), {2}: (7, {})} | custom-call | tf_op jit(solution)/shard_map/update/pallas_call | solution.py:206
  98.1 5.9 %reshape.108 = bf16[8,4,384,40]{3,2,1,0:T(8,128)(2,1)S(1)} reshape(bf16[3840,128]{1,0:T(8,128)(2,1)} %get-tuple-element.49) | data formatting | bytes 1966080 | tf_op jit(solution)/shard_map/reshape | solution.py:264
  104.1 3.1 %all-to-all-done.1 = bf16[4,8,80,352]{3,2,1,0:T(8,128)(2,1)} async-done(((bf16[4,8,80,352]{3,2,1,0:T(8,128)(2,1)}), bf16[4,8,80,352]{3,2,1,0:T(8,128)(2,1)}, u32[]{:S(2)}, u32[]{:S(2)}) %all-to-all-start.1) | async-done | bytes 1802272 | tf_op jit(solution)/shard_map/all_to_all | solution.py:149
  109.4 3.7 %all-to-all-start.2 = ((bf16[4,8,40,384]{3,2,1,0:T(8,128)(2,1)}), bf16[4,8,40,384]{3,2,1,0:T(8,128)(2,1)S(1)}, u32[]{:S(2)}, u32[]{:S(2)}) async-start(bf16[4,8,40,384]{3,2,1,0:T(8,128)(2,1)} %copy.61), calls=%async_computation.2 | async-start | bytes 1966080 | tf_op jit(solution)/shard_map/all_to_all | solution.py:149
  114.9 4.3 %reshape.96.gradient_ref = bf16[7040,128]{1,0:T(8,128)(2,1)} reshape(bf16[8,4,80,352]{3,2,1,0:T(8,128)(2,1)S(1)} %copy.57) | data formatting | bytes 3604480 | tf_op jit(solution)/shard_map/reshape | solution.py:254
  119.3 13.3 %update.5 = (f32[12160,128]{1,0:T(8,128)}, f32[12160,128]{1,0:T(8,128)}, f32[12160,128]{1,0:T(8,128)}, bf16[7040,128]{1,0:T(8,128)(2,1)}) custom-call(f32[1,1]{1,0:T(1,128)} %min.3.scale_ref, bf16[7040,128]{1,0:T(8,128)(2,1)} %reshape.96.gradient_ref, f32[12160,128]{1,0:T(8,128)} %bitcast.71, ...), custom_call_target="tpu_custom_call", output_to_operand_aliasing={{0}: (5, {}), {1}: (6, {}), {2}: (7, {})} | custom-call | tf_op jit(solution)/shard_map/update/pallas_call | solution.py:206
  132.5 3.9 %reshape.107 = bf16[8,4,80,352]{3,2,1,0:T(8,128)(2,1)S(1)} reshape(bf16[7040,128]{1,0:T(8,128)(2,1)} %get-tuple-element.48) | data formatting | bytes 3604480 | tf_op jit(solution)/shard_map/reshape | solution.py:264
  137.9 4.3 %all-to-all-start.3 = ((bf16[4,8,80,352]{3,2,1,0:T(8,128)(2,1)}), bf16[4,8,80,352]{3,2,1,0:T(8,128)(2,1)S(1)}, u32[]{:S(2)}, u32[]{:S(2)}) async-start(bf16[4,8,80,352]{3,2,1,0:T(8,128)(2,1)} %bitcast.85), calls=%async_computation.3 | async-start | bytes 3932160 | tf_op jit(solution)/shard_map/all_to_all | solution.py:149
  149.7 3.4 %multiply_add_fusion.1 = (f32[8,768,160]{1,2,0:T(8,128)}, bf16[8,768,160]{1,2,0:T(8,128)(2,1)}) fusion(f32[8,768,160]{1,2,0:T(8,128)S(1)} %copy-done.3, bf16[8,384,160]{1,2,0:T(8,128)(2,1)S(1)} %get-tuple-element.66, bf16[8,384,160]{1,2,0:T(8,128)(2,1)S(1)} %get-tuple-element.65), kind=kLoop, calls=%fused_computation.1 | loop fusion | flops 7864320 | bytes 11796480 | tf_op jit(solution)/shard_map/add | solution.py:272
  153.1 34.1 %all-to-all-done.3 = bf16[4,8,80,352]{3,2,1,0:T(8,128)(2,1)S(1)} async-done(((bf16[4,8,80,352]{3,2,1,0:T(8,128)(2,1)}), bf16[4,8,80,352]{3,2,1,0:T(8,128)(2,1)S(1)}, u32[]{:S(2)}, u32[]{:S(2)}) %all-to-all-start.3) | async-done | bytes 1802272 | tf_op jit(solution)/shard_map/all_to_all | solution.py:149
  188.5 3.5 %all-to-all-start.4 = ((bf16[4,1,40,1024]{3,2,1,0:T(8,128)(2,1)}), bf16[4,1,40,1024]{3,2,1,0:T(8,128)(2,1)S(1)}, u32[]{:S(2)}, u32[]{:S(2)}) async-start(bf16[4,1,40,1024]{3,2,1,0:T(8,128)(2,1)} %copy.64), calls=%async_computation.4 | async-start | bytes 655360 | tf_op jit(solution)/shard_map/all_to_all | solution.py:149
  192.0 3.1 %copy.62 = bf16[8,80,4,352]{3,2,1,0:T(4,128)(2,1)S(1)} copy(bf16[8,80,4,352]{3,1,0,2:T(8,128)(2,1)} %bitcast.84) | data formatting | bytes 3604480 | tf_op jit(solution)/shard_map/transpose | solution.py:179
  208.2 7.0 %multiply_add_fusion = (f32[8,160,1408]{2,1,0:T(8,128)}, bf16[8,160,1408]{2,1,0:T(8,128)(2,1)}) fusion(f32[8,160,1408]{2,1,0:T(8,128)} %param.20, bf16[8,80,1408]{2,1,0:T(8,128)(2,1)S(1)} %get-tuple-element.64, bf16[8,80,1408]{2,1,0:T(8,128)(2,1)S(1)} %get-tuple-element.63), kind=kLoop, calls=%fused_computation | loop fusion | flops 14417920 | bytes 21626880 | tf_op jit(solution)/shard_map/add | solution.py:272
  (77 shorter events, 57.5 us)
Async XLA Ops:
  3.7 4.1 %collective-permute-start = (bf16[8,384,160]{1,2,0:T(8,128)(2,1)}, bf16[8,384,160]{1,2,0:T(8,128)(2,1)S(1)}, u32[]{:S(2)}, u32[]{:S(2)}) collective-permute-start(bf16[8,384,160]{1,2,0:T(8,128)(2,1)} %get-tuple-element.67), channel_id=1, source_target_pairs={{0,16},{16,0},{1,17},{17,1},{2,18},{18,2},{3,19},{19,3},{4,20},{20... | collective-permute-start | bytes 2949128 | tf_op jit(solution)/shard_map/ppermute | solution.py:50
  4.5 10.0 %collective-permute-start.1 = (bf16[1,1024,160]{1,2,0:T(8,128)(2,1)S(1)}, bf16[1,1024,160]{1,2,0:T(8,128)(2,1)S(1)}, u32[]{:S(2)}, u32[]{:S(2)}) collective-permute-start(bf16[1,1024,160]{1,2,0:T(8,128)(2,1)S(1)} %get-tuple-element.71), channel_id=1, source_target_pairs={{0,16},{16,0},{1,17},{17,1},{2,18},{18,2},{3,19},{19,3},{4,20},{20... | collective-permute-start | bytes 983048 | tf_op jit(solution)/shard_map/ppermute | solution.py:50
  7.8 18.2 %collective-permute-start.2 = (bf16[8,80,1408]{2,1,0:T(8,128)(2,1)}, bf16[8,80,1408]{2,1,0:T(8,128)(2,1)S(1)}, u32[]{:S(2)}, u32[]{:S(2)}) collective-permute-start(bf16[8,80,1408]{2,1,0:T(8,128)(2,1)} %dynamic-slice_bitcast_fusion), channel_id=1, source_target_pairs={{0,16},{16,0},{1,17},{17,1},{2,18},{18,2},{3,19},{19,3},{4,20},{20... | collective-permute-start | bytes 5406728 | tf_op jit(solution)/shard_map/ppermute | solution.py:50
  15.2 8.3 %copy-start.10 = (f32[8,1,384]{2,1,0:T(1,128)S(1)}, f32[8,1,384]{2,1,0:T(1,128)}, u32[]{:S(2)}) copy-start(f32[8,1,384]{2,1,0:T(1,128)} %get-tuple-element.33) | copy-start | bytes 36868
  17.3 6.8 %copy-start.11 = (f32[1,1,1024]{2,1,0:T(1,128)S(1)}, f32[1,1,1024]{2,1,0:T(1,128)}, u32[]{:S(2)}) copy-start(f32[1,1,1024]{2,1,0:T(1,128)} %get-tuple-element.35) | copy-start | bytes 12292
  17.3 38.6 %all-to-all-start = ((bf16[4,32,40,128]{3,2,1,0:T(8,128)(2,1)}), bf16[4,32,40,128]{3,2,1,0:T(8,128)(2,1)S(1)}, u32[]{:S(2)}, u32[]{:S(2)}) async-start(bf16[4,32,40,128]{3,2,1,0:T(8,128)(2,1)} %get-tuple-element.36), calls=%async_computation | async-start | bytes 2621440 | tf_op jit(solution)/shard_map/all_to_all | solution.py:149
  30.9 5.7 %collective-permute-start.3 = (f32[1,1]{1,0:T(1,128)}, f32[1,1]{1,0:T(1,128)}, u32[]{:S(2)}, u32[]{:S(2)}) collective-permute-start(f32[1,1]{1,0:T(1,128)} %bitcast.8), channel_id=1, source_target_pairs={{0,16},{16,0},{1,17},{17,1},{2,18},{18,2},{3,19},{19,3},{4,20},{20... | collective-permute-start | bytes 20 | tf_op jit(solution)/shard_map/ppermute | solution.py:50
  37.1 12.3 %collective-permute-start.4 = (f32[1,1]{1,0:T(1,128)}, f32[1,1]{1,0:T(1,128)}, u32[]{:S(2)}, u32[]{:S(2)}) collective-permute-start(f32[1,1]{1,0:T(1,128)} %add.91), channel_id=1, source_target_pairs={{0,4},{4,0},{8,12},{12,8},{1,5},{5,1},{9,13},{13,9},{2,6},{6,2},{1... | collective-permute-start | bytes 20 | tf_op jit(solution)/shard_map/ppermute | solution.py:50
  44.9 9.7 %collective-permute-start.5 = (f32[1,1]{1,0:T(1,128)}, f32[1,1]{1,0:T(1,128)}, u32[]{:S(2)}, u32[]{:S(2)}) collective-permute-start(f32[1,1]{1,0:T(1,128)} %add.91), channel_id=1, source_target_pairs={{0,8},{4,12},{8,0},{12,4},{1,9},{5,13},{9,1},{13,5},{2,10},{6,14},... | collective-permute-start | bytes 20 | tf_op jit(solution)/shard_map/ppermute | solution.py:50
  45.7 9.0 %collective-permute-start.6 = (f32[1,1]{1,0:T(1,128)}, f32[1,1]{1,0:T(1,128)}, u32[]{:S(2)}, u32[]{:S(2)}) collective-permute-start(f32[1,1]{1,0:T(1,128)} %add.91), channel_id=1, source_target_pairs={{0,12},{4,8},{8,4},{12,0},{1,13},{5,9},{9,5},{13,1},{2,14},{6,10},... | collective-permute-start | bytes 20 | tf_op jit(solution)/shard_map/ppermute | solution.py:50
  55.9 18.7 %copy-start.2 = (bf16[4,32,40,128]{3,2,1,0:T(8,128)(2,1)}, bf16[4,32,40,128]{3,2,1,0:T(8,128)(2,1)S(1)}, u32[]{:S(2)}) copy-start(bf16[4,32,40,128]{3,2,1,0:T(8,128)(2,1)S(1)} %all-to-all-done) | copy-start | bytes 3932164
  57.6 49.6 %all-to-all-start.1 = ((bf16[4,8,80,352]{3,2,1,0:T(8,128)(2,1)}), bf16[4,8,80,352]{3,2,1,0:T(8,128)(2,1)}, u32[]{:S(2)}, u32[]{:S(2)}) async-start(bf16[4,8,80,352]{3,2,1,0:T(8,128)(2,1)} %copy.56), calls=%async_computation.1 | async-start | bytes 3932160 | tf_op jit(solution)/shard_map/all_to_all | solution.py:149
  62.2 2.2 %collective-permute-start.10 = (bf16[8,3072]{1,0:T(8,128)(2,1)S(1)}, bf16[8,3072]{1,0:T(8,128)(2,1)S(1)}, u32[]{:S(2)}, u32[]{:S(2)}) collective-permute-start(bf16[8,3072]{1,0:T(8,128)(2,1)S(1)} %bitcast.94), channel_id=1, source_target_pairs={{0,16},{16,0},{1,17},{17,1},{2,18},{18,2},{3,19},{19,3},{4,20},{20... | collective-permute-start | bytes 147464 | tf_op jit(solution)/shard_map/ppermute | solution.py:50
  65.0 4.8 %collective-permute-start.7 = (f32[1,1]{1,0:T(1,128)}, f32[1,1]{1,0:T(1,128)}, u32[]{:S(2)}, u32[]{:S(2)}) collective-permute-start(f32[1,1]{1,0:T(1,128)} %add.94), channel_id=1, source_target_pairs={{0,1},{1,0},{2,3},{3,2},{4,5},{5,4},{6,7},{7,6},{8,9},{9,8},{10,11... | collective-permute-start | bytes 20 | tf_op jit(solution)/shard_map/ppermute | solution.py:50
  67.0 3.6 %collective-permute-start.8 = (f32[1,1]{1,0:T(1,128)}, f32[1,1]{1,0:T(1,128)}, u32[]{:S(2)}, u32[]{:S(2)}) collective-permute-start(f32[1,1]{1,0:T(1,128)} %add.94), channel_id=1, source_target_pairs={{0,2},{1,3},{2,0},{3,1},{4,6},{5,7},{6,4},{7,5},{8,10},{9,11},{10,... | collective-permute-start | bytes 20 | tf_op jit(solution)/shard_map/ppermute | solution.py:50
  68.9 3.7 %collective-permute-start.9 = (f32[1,1]{1,0:T(1,128)}, f32[1,1]{1,0:T(1,128)}, u32[]{:S(2)}, u32[]{:S(2)}) collective-permute-start(f32[1,1]{1,0:T(1,128)} %add.94), channel_id=1, source_target_pairs={{0,3},{1,2},{2,1},{3,0},{4,7},{5,6},{6,5},{7,4},{8,11},{9,10},{10,... | collective-permute-start | bytes 20 | tf_op jit(solution)/shard_map/ppermute | solution.py:50
  109.4 28.5 %all-to-all-start.2 = ((bf16[4,8,40,384]{3,2,1,0:T(8,128)(2,1)}), bf16[4,8,40,384]{3,2,1,0:T(8,128)(2,1)S(1)}, u32[]{:S(2)}, u32[]{:S(2)}) async-start(bf16[4,8,40,384]{3,2,1,0:T(8,128)(2,1)} %copy.61), calls=%async_computation.2 | async-start | bytes 1966080 | tf_op jit(solution)/shard_map/all_to_all | solution.py:149
  137.9 49.3 %all-to-all-start.3 = ((bf16[4,8,80,352]{3,2,1,0:T(8,128)(2,1)}), bf16[4,8,80,352]{3,2,1,0:T(8,128)(2,1)S(1)}, u32[]{:S(2)}, u32[]{:S(2)}) async-start(bf16[4,8,80,352]{3,2,1,0:T(8,128)(2,1)} %bitcast.85), calls=%async_computation.3 | async-start | bytes 3932160 | tf_op jit(solution)/shard_map/all_to_all | solution.py:149
  143.3 4.5 %collective-permute-start.12 = (bf16[8,384,160]{1,2,0:T(8,128)(2,1)}, bf16[8,384,160]{1,2,0:T(8,128)(2,1)}, u32[]{:S(2)}, u32[]{:S(2)}) collective-permute-start(bf16[8,384,160]{1,2,0:T(8,128)(2,1)} %bitcast.27), channel_id=1, source_target_pairs={{0,16},{16,0},{1,17},{17,1},{2,18},{18,2},{3,19},{19,3},{4,20},{20... | collective-permute-start | bytes 2949128 | tf_op jit(solution)/shard_map/ppermute | solution.py:50
  187.2 4.8 %copy-start = (bf16[4,8,80,352]{3,2,1,0:T(8,128)(2,1)}, bf16[4,8,80,352]{3,2,1,0:T(8,128)(2,1)S(1)}, u32[]{:S(2)}) copy-start(bf16[4,8,80,352]{3,2,1,0:T(8,128)(2,1)S(1)} %all-to-all-done.3) | copy-start | bytes 5406724
  188.5 12.1 %all-to-all-start.4 = ((bf16[4,1,40,1024]{3,2,1,0:T(8,128)(2,1)}), bf16[4,1,40,1024]{3,2,1,0:T(8,128)(2,1)S(1)}, u32[]{:S(2)}, u32[]{:S(2)}) async-start(bf16[4,1,40,1024]{3,2,1,0:T(8,128)(2,1)} %copy.64), calls=%async_computation.4 | async-start | bytes 655360 | tf_op jit(solution)/shard_map/all_to_all | solution.py:149
  197.4 8.5 %copy-start.4 = (f32[2048,160]{0,1:T(8,128)S(1)}, f32[2048,160]{0,1:T(8,128)}, u32[]{:S(2)}) copy-start(f32[2048,160]{0,1:T(8,128)} %param.22) | copy-start | bytes 3932164
  197.4 9.7 %collective-permute-start.11 = (bf16[8,80,1408]{2,1,0:T(8,128)(2,1)}, bf16[8,80,1408]{2,1,0:T(8,128)(2,1)S(1)}, u32[]{:S(2)}, u32[]{:S(2)}) collective-permute-start(bf16[8,80,1408]{2,1,0:T(8,128)(2,1)} %reshape.109), channel_id=1, source_target_pairs={{0,16},{16,0},{1,17},{17,1},{2,18},{18,2},{3,19},{19,3},{4,20},{20... | collective-permute-start | bytes 5406728 | tf_op jit(solution)/shard_map/ppermute | solution.py:50
  200.6 4.3 %collective-permute-start.13 = (bf16[1,1024,160]{1,2,0:T(8,128)(2,1)S(1)}, bf16[1,1024,160]{1,2,0:T(8,128)(2,1)S(1)}, u32[]{:S(2)}, u32[]{:S(2)}) collective-permute-start(bf16[1,1024,160]{1,2,0:T(8,128)(2,1)S(1)} %bitcast.90), channel_id=1, source_target_pairs={{0,16},{16,0},{1,17},{17,1},{2,18},{18,2},{3,19},{19,3},{4,20},{20... | collective-permute-start | bytes 983048 | tf_op jit(solution)/shard_map/ppermute | solution.py:50
  (7 other events, 17.1 us)
